TPU v7x, 128 devices: a whole 4x4x4 slice. The times are simulated.
128 devices in a mesh: orb: 16 (over x_hi, z, core), grp: 8 (over x_lo, y).
Axes of the slice: x: 4 (x_hi: 2, x_lo: 2; x = x_hi * 2 + x_lo), y: 4, z: 4, core: 2. Of those that a mesh axis runs over, the one named last changes fastest.
Arguments:
- orbitals: float32 [1024, 64, 4096], P(('orb', 'grp')), may hold values from -5 to 5
- occupations: float32 [1024], P(('orb', 'grp')), may hold values from 0.5 to 2
- external: float32 [64, 4096], P('orb'), may hold values from -1.5 to 0.5
Outputs:
- applied: float32 [1024, 64, 4096], P(('orb', 'grp'))
All inputs are finite; a program needn't handle non-finite values.
Results may differ from a plain program's by a relative error of at most 0.0001.
Values sent between devices are 32-bit elements; how exact they have to be, the bound alone decides.
No kernel may reach another device: no remote copies, remote signals or barrier semaphores. Data moves between devices by JAX's collectives and lax.ppermute only.
A program may use at most 256 MiB of HBM per device.

v0:
```python
import functools
import math

import jax
import jax.numpy as jnp
import ml_dtypes
import numpy as np
from jax import lax
from jax.experimental import pallas as pl
from jax.experimental.pallas import tpu as pltpu
from jax.sharding import Mesh, PartitionSpec as P

MAGIC_TAPS = [
    8.433424733352934e-07,
    -1.290557201342061e-05,
    8.76298447621056e-05,
    -0.00030158038132690465,
    0.001747237136729939,
    -0.009420470302010804,
    0.023738214637249424,
    0.0612625895831208,
    0.9940415697834003,
    -0.06048952891969835,
    -0.021030251609303816,
    0.013372634148547948,
    -0.0034412814449349387,
    0.0004944322768868992,
    -5.185986881173433e-05,
    2.7273449291197967e-06,
]
KINETIC_HALF = [
    -3.55369228991319,
    2.2191465938911166,
    -0.615614146557007,
    0.23717805821538057,
    -0.08226639997421234,
    0.022070291884822554,
    -0.004097656893426338,
    0.00045167920287502236,
    -2.3982285245075998e-05,
    2.0904234952920368e-06,
    -3.7230763047369276e-07,
    -1.0585705549674146e-08,
    -5.8138798302825403e-11,
    2.7080049362631943e-13,
    -6.9244749406392e-18,
]
KINETIC_TAPS = KINETIC_HALF[:0:-1] + KINETIC_HALF
SPACING = 0.45

N = 64
GROUP = 4
ROWS = GROUP * N
PAIRS = N // 2
BF16 = ml_dtypes.bfloat16
AXES = ("xh", "z", "core", "xl", "y")
CHIPS = ("xh", "xl", "y", "z")
PARAMS = dict(vmem_limit_bytes=60 * 2**20)
UNROLL = 16


def circulant(taps, offset):
    matrix = np.zeros((N, N), np.float32)
    for position, weight in enumerate(taps):
        for row in range(N):
            matrix[row, (row + position - offset) % N] += np.float32(weight)
    return matrix


def halves(matrix):
    high = matrix.astype(BF16)
    return high, (matrix - high.astype(np.float32)).astype(BF16)


MIXED = np.arange(128).reshape(2, 16, 4).transpose(1, 0, 2).reshape(128)


def lane_operator(matrix, order=slice(None)):
    return np.concatenate([np.concatenate([part, part], 1)[order] for part in halves(np.kron(np.eye(2, dtype=np.float32), matrix))])


def slow_operator(matrix):
    return np.concatenate(halves(np.kron(matrix, np.eye(4, dtype=np.float32))))


MAGIC = circulant(MAGIC_TAPS, 8)
KINETIC = circulant(KINETIC_TAPS, 14) * np.float32(-0.5 / (SPACING * SPACING))
CENTRE = float(np.float32(3.0) * KINETIC[0, 0])
SIDES = KINETIC - np.diag(np.diag(KINETIC))
ONE = np.eye(N, dtype=np.float32)


def split(block):
    high = block.astype(jnp.bfloat16)
    return high, (block - high.astype(jnp.float32)).astype(jnp.bfloat16)


def both(block):
    return jnp.concatenate(split(block), axis=1)


def run(jobs):
    queues = []
    for unit, queue in enumerate(jobs):
        steps = []
        for index, (parts, accs, finish) in enumerate(queue):
            for at, part in enumerate(parts):
                steps.append((part, accs, finish if at == len(parts) - 1 else None))
        queues.append(steps)
    pending = [None] * len(queues)

    def push(unit, at):
        (operand, transpose, _), _, _ = queues[unit][at]
        pltpu.matmul_push_rhs(operand(), at % 2, unit, transpose=transpose)

    for unit in range(len(queues)):
        push(unit, 0)
    for at in range(len(queues[0])):
        for unit, queue in enumerate(queues):
            if at + 1 < len(queue):
                push(unit, at + 1)
            (_, _, products), accs, finish = queue[at]
            for which, (acc, left) in enumerate(products):
                pltpu.matmul_acc_lhs(accs[acc], left(), load_staged_rhs=at % 2 if which == 0 else None)
            if pending[unit] is not None:
                done, held = pending[unit]
                done(*[pltpu.matmul_pop(acc) for acc in held])
                pending[unit] = None
            if finish is not None:
                pending[unit] = (finish, accs)
    for done, held in pending:
        done(*[pltpu.matmul_pop(acc) for acc in held])


def part(ref, start, size):
    return lambda: ref[start : start + size]


def lanes_at(index, size):
    return pl.ds(pl.multiple_of(index * size, size), size)


def along_tiles(operand, products, accs, target):
    def step(index, _):
        def job(tile, unit, at):
            def finish(*outs):
                for ref, out in zip(target, outs):
                    ref[tile] = out.reshape(16, 8, ROWS)

            return ([(lambda: operand(tile), True, products)], accs[unit][at % 2], finish)

        run([[job(index * UNROLL + 2 * at + unit, unit, at) for at in range(UNROLL // 2)] for unit in range(2)])
        return 0

    lax.fori_loop(0, PAIRS // UNROLL, step, 0)


def along_slow(source, target, op_ref, accs, add=None):
    def step(index, _):
        def job(block, unit, at):
            cache = []

            def high():
                cache.extend(split(source[:, block].reshape(256, ROWS)))
                return cache[0]

            def finish(out):
                out = out.reshape(PAIRS, 8, ROWS)
                target[:, block] = out if add is None else out + add[:, block]

            first = (high, False, [(0, part(op_ref, 0, 256)), (0, part(op_ref, 256, 256))])
            second = (lambda: cache[1], False, [(0, part(op_ref, 0, 256))])
            return ([first, second], [accs[unit][at % 2]], finish)

        run([[job(index * 8 + 2 * at + unit, unit, at) for at in range(4)] for unit in range(2)])
        return 0

    lax.fori_loop(0, 2, step, 0)


def natural(ref, index, pair):
    rows = []
    for tile in range(2):
        block = ref[index * 2 + tile, :, :, pair * 128 : pair * 128 + 128].reshape(8, 2, 8, 128)
        even, odd = block[:, 0], block[:, 1]
        upper = lax.broadcasted_iota(jnp.int32, even.shape, 1) < 4
        rows.append(jnp.where(upper, even, pltpu.roll(odd, 4, 1)).reshape(N, 128))
        rows.append(jnp.where(upper, pltpu.roll(even, 4, 1), odd).reshape(N, 128))
    return jnp.concatenate(rows, axis=0)


def along_x(steps_of, accs, finish_of, after):
    count = UNROLL // 2

    def step(index, _):
        def job(block, unit, at):
            return (steps_of(block, unit), [accs[unit][at % 2][0]], functools.partial(finish_of, block, unit))

        run([[job(index * count + at, unit, at) for at in range(count)] for unit in range(2)])
        if after is not None:
            for at in range(count):
                after(index * count + at)
        return 0

    lax.fori_loop(0, 16 // count, step, 0)


def chunks(core):
    for position in range(64):
        xh, xl, y, z = position // 32, position // 16 % 2, position // 4 % 4, position % 4
        member = xl * 4 + y
        plane = xh * 32 + z * 8 + member // 2
        yield position, plane + core * 4, plane + 4 - core * 4, member % 2


def forward_kernel(core_ref, occ_ref, z_ref, y_ref, x_ref, orb_ref, val_ref, keep_ref, send_ref, first, second, total, spread, *accs):
    group = pl.program_id(0)
    small, large = ((accs[0:1], accs[1:2]), (accs[2:3], accs[3:4])), (accs[4:6], accs[6:8])
    z_products = [(0, part(z_ref, 0, 128)), (0, part(z_ref, 128, 128))]
    x_products = [(0, part(x_ref, 0, 128)), (0, part(x_ref, 128, 128))]
    along_tiles(lambda tile: both(orb_ref[:, :, lanes_at(tile, 128)].reshape(ROWS, 128)), z_products, small, [first])
    along_slow(first, second, y_ref, large)

    @pl.when(group == 0)
    def _():
        total[...] = jnp.zeros_like(total)

    def finish(block, pair, out):
        lanes = lanes_at(block, 256)
        out = out.reshape(2, N, 256)
        val_ref[pair * 2 : pair * 2 + 2, :, lanes] = out
        weighted = [occ_ref[group * GROUP + pair * 2 + one] * (out[one] * out[one]) for one in range(2)]
        total[:, lanes] = total[:, lanes] + (weighted[0] + weighted[1])

    along_x(lambda block, pair: [(lambda: both(natural(second, block, pair)), True, x_products)], small, finish, None)

    @pl.when(group == pl.num_programs(0) - 1)
    def _():
        for tile in range(32):
            spread[pl.ds(tile, N, stride=32), :] = total[:, tile * 128 : tile * 128 + 128]
        for position, here, there, half in chunks(core_ref[0]):
            keep_ref[position] = spread[pl.ds(pl.multiple_of(here * 32 + half * 16, 16), 16), :]
            send_ref[position] = spread[pl.ds(pl.multiple_of(there * 32 + half * 16, 16), 16), :]


def back_kernel(core_ref, z_ref, y_ref, x_ref, own_ref, other_ref, val_ref, kin0_ref, kin1_ref, out_ref, first, second, total, spread, *accs):
    group = pl.program_id(0)
    small, large = ((accs[0:1], accs[1:2]), (accs[2:3], accs[3:4])), (accs[4:6], accs[6:8])
    z_products = [(0, part(z_ref, 0, 128)), (0, part(z_ref, 128, 128))]
    x_products = [(0, part(x_ref, 0, 128)), (0, part(x_ref, 128, 128))]

    @pl.when(group == 0)
    def _():
        for position, here, there, half in chunks(core_ref[0]):
            spread[pl.ds(pl.multiple_of(here * 32 + half * 16, 16), 16), :] = own_ref[position]
            spread[pl.ds(pl.multiple_of(there * 32 + half * 16, 16), 16), :] = other_ref[position]
        for tile in range(32):
            total[:, tile * 128 : tile * 128 + 128] = spread[pl.ds(tile, N, stride=32), :]

    def weighted(tile):
        lanes = lanes_at(tile, 128)
        return both((val_ref[:, :, lanes] * total[:, lanes][None]).reshape(ROWS, 128))

    along_tiles(weighted, z_products, small, [first])
    along_slow(first, second, y_ref, large)

    for which, kin_ref in enumerate((kin0_ref, kin1_ref)):

        @pl.when(group == which)
        def _():
            def finish(block, pair, out):
                at = (slice(pair * 2, pair * 2 + 2), slice(None), lanes_at(block, 256))
                out_ref[at] = out.reshape(2, N, 256) + kin_ref[at]

            along_x(lambda block, pair: [(lambda: both(natural(second, block, pair)), True, x_products)], small, finish, None)


def kinetic_kernel(_, z_ref, y_ref, x_ref, orb_ref, out_ref, first, second, *accs):
    small, large = ((accs[0:2], accs[2:4]), (accs[4:6], accs[6:8])), (accs[8:10], accs[10:12])
    z_products = [(0, part(z_ref, 0, 128)), (1, part(z_ref, 128, 128)), (1, part(z_ref, 256, 128))]
    one_products = [(0, part(x_ref, 0, 128))]
    x_products = [(0, part(x_ref, 128, 128)), (0, part(x_ref, 256, 128))]
    along_tiles(lambda tile: both(orb_ref[:, :, lanes_at(tile, 128)].reshape(ROWS, 128)), z_products, small, [first, second])
    along_slow(first, second, y_ref, large, second)

    def steps(block, pair):
        return [
            (lambda: both(natural(second, block, pair)), True, one_products),
            (lambda: both(natural(first, block, pair)), True, x_products),
        ]

    def finish(block, pair, out):
        at = (slice(pair * 2, pair * 2 + 2), slice(None), lanes_at(block, 256))
        out_ref[at] = out.reshape(2, N, 256) + CENTRE * orb_ref[at]

    along_x(steps, small, finish, None)


SMEM = pl.BlockSpec(memory_space=pltpu.SMEM)
ORBITALS = pl.BlockSpec((GROUP, N, N * N), lambda group: (group, 0, 0))
TURNED = pltpu.VMEM((PAIRS, 16, 8, ROWS), jnp.float32)
PLANES = pltpu.VMEM((N, N * N), jnp.float32)
SPREAD = pltpu.VMEM((N * 32, 128), jnp.float32)
HALF = jax.ShapeDtypeStruct((64, 16, 128), jnp.float32)
ONE_ROWS = lane_operator(ONE)[:128]


def scoped(kernel, accs):
    return lambda *refs: pl.run_scoped(functools.partial(kernel, *refs), *accs)


def accs_for(*counts):
    small, large = counts
    return [pltpu.ACC(unit)((128, 256), jnp.float32) for unit in range(2) for _ in range(small)] + [
        pltpu.ACC(unit)((256, 256), jnp.float32) for unit in range(2) for _ in range(large)
    ]


def whole(shape):
    return pl.BlockSpec(shape, lambda *_: (0,) * len(shape), pipeline_mode=pl.Buffered(1))


def cost(rows, bytes_accessed):
    return pl.CostEstimate(flops=rows * 2 * 256 * 256, bytes_accessed=bytes_accessed, transcendentals=0)


def constants(*tables):
    return [whole(table.shape) for table in tables], [jnp.asarray(table) for table in tables]


def forward(core, occupations, orbitals):
    count = orbitals.shape[0]
    specs, tables = constants(lane_operator(MAGIC, MIXED), slow_operator(MAGIC), lane_operator(MAGIC))
    return pl.pallas_call(
        scoped(forward_kernel, accs_for(2, 2)),
        grid=(count // GROUP,),
        in_specs=[SMEM, SMEM, *specs, ORBITALS],
        out_specs=[ORBITALS, whole(HALF.shape), whole(HALF.shape)],
        out_shape=[jax.ShapeDtypeStruct(orbitals.shape, jnp.float32), HALF, HALF],
        scratch_shapes=[TURNED, TURNED, PLANES, SPREAD],
        compiler_params=pltpu.CompilerParams(**PARAMS),
        cost_estimate=cost(57344, 18 * 2**20),
        name="forward",
    )(core, occupations, *tables, orbitals)


def back(core, own, other, values, kin0, kin1):
    count = values.shape[0]
    specs, tables = constants(lane_operator(MAGIC.T, MIXED), slow_operator(MAGIC.T), lane_operator(MAGIC.T))
    quad = whole((GROUP, N, N * N))
    return pl.pallas_call(
        scoped(back_kernel, accs_for(2, 2)),
        grid=(count // GROUP,),
        in_specs=[SMEM, *specs, whole(HALF.shape), whole(HALF.shape), ORBITALS, quad, quad],
        out_specs=ORBITALS,
        out_shape=jax.ShapeDtypeStruct(values.shape, jnp.float32),
        scratch_shapes=[TURNED, TURNED, PLANES, SPREAD],
        compiler_params=pltpu.CompilerParams(**PARAMS),
        cost_estimate=cost(57344, 26 * 2**20),
        name="back",
    )(core, *tables, own, other, values, kin0, kin1)


def kinetic(after, orbitals, group):
    block = (GROUP, N, N * N)
    z_table = np.concatenate([ONE_ROWS[MIXED], lane_operator(SIDES, np.arange(128)[MIXED])])
    x_table = np.concatenate([ONE_ROWS, lane_operator(SIDES)])
    specs, tables = constants(z_table, slow_operator(SIDES), x_table)
    return pl.pallas_call(
        scoped(kinetic_kernel, accs_for(4, 2)),
        grid=(1,),
        in_specs=[SMEM, *specs, pl.BlockSpec(block, lambda _: (group, 0, 0))],
        out_specs=pl.BlockSpec(block, lambda _: (0, 0, 0)),
        out_shape=jax.ShapeDtypeStruct(block, jnp.float32),
        scratch_shapes=[TURNED, TURNED],
        compiler_params=pltpu.CompilerParams(**PARAMS),
        cost_estimate=cost(49152, 9 * 2**20),
        name=f"kinetic{group}",
    )(after, *tables, orbitals)


SWAP = [(0, 1), (1, 0)]


def on_device(orbitals, occupations, external):
    core = lax.axis_index("core").astype(jnp.int32).reshape(1)
    member = lax.axis_index("xl") * 4 + lax.axis_index("y")
    own_external = lax.dynamic_index_in_dim(external.reshape(8, 16, 128), member, 0, keepdims=False)
    values, keep, send = forward(core, occupations, orbitals)
    partial = keep + lax.ppermute(send, "core", SWAP)
    partial, after = lax.optimization_barrier((partial, core))
    shares = lax.all_to_all(partial, CHIPS, 0, 0, tiled=True)
    shares, kin0 = lax.optimization_barrier((shares, kinetic(after, orbitals, 0)))
    density = jnp.sum(shares, axis=0)
    potential = own_external - jnp.cbrt(3.0 / math.pi * density)
    copies, after = lax.optimization_barrier((jnp.broadcast_to(potential[None], (64, 16, 128)), core))
    own = lax.all_to_all(copies, CHIPS, 0, 0, tiled=True)
    own, kin1 = lax.optimization_barrier((own, kinetic(after, orbitals, 1)))
    other = lax.ppermute(own, "core", SWAP)
    return back(core, own, other, values, kin0, kin1)


def solution(mesh):
    fine = Mesh(mesh.devices.reshape(2, 4, 2, 2, 4), AXES)
    orb = ("xh", "z", "core")
    return jax.shard_map(
        on_device,
        mesh=fine,
        in_specs=(P(AXES, None, None), P(AXES), P(orb, None)),
        out_specs=P(AXES, None, None),
        check_vma=False,
    )
```

profile of v0, /device:TPU:1, one launch (start us, length us, event | category | flops | bytes accessed | tf_op | source)
XLA Modules:
  0.0 90.4 jit_solution(580382396611841001)
XLA Ops:
  0.0 0.0 copy-start.1
  0.0 16.8 %forward.1 = (f32[8,64,4096]{2,1,0:T(8,128)}, f32[64,16,128]{2,1,0:T(8,128)}, f32[64,16,128]{2,1,0:T(8,128)}) custom-call(s32[1]{0:T(128)} %bitcast.refs_0_, f32[8]{0:T(128)} %refs_1_.4, bf16[256,256]{1,0:T(8,128)(2,1)} %constant.42.clone.refs_2_, bf16[512,256]{1,0:T(8,128)(2,1)} %constant.43.clone.refs_3_, bf16[256,256]{1,0:T(8,128)(2,1)} %constant.44.clone.refs_4_, ...), custom_call_target="tpu_custom_call" | custom-call | flops 7516192768 | bytes 18874368 | tf_op jit(solution)/shard_map/forward/pallas_call | solution.py:334
  16.8 1.4 %collective-permute-start = (f32[64,16,128]{2,1,0:T(8,128)}, f32[64,16,128]{2,1,0:T(8,128)S(1)}, u32[]{:S(2)}, u32[]{:S(2)}) collective-permute-start(f32[64,16,128]{2,1,0:T(8,128)} %get-tuple-element.17), channel_id=1, source_target_pairs={{0,8},{8,0},{1,9},{9,1},{2,10},{10,2},{3,11},{11,3},{4,12},{12,4},... | collective-permute-start | bytes 1572872 | tf_op jit(solution)/shard_map/ppermute | solution.py:390
  18.2 0.0 copy-done.1
  18.2 1.7 %collective-permute-done = f32[64,16,128]{2,1,0:T(8,128)S(1)} collective-permute-done((f32[64,16,128]{2,1,0:T(8,128)}, f32[64,16,128]{2,1,0:T(8,128)S(1)}, u32[]{:S(2)}, u32[]{:S(2)}) %collective-permute-start) | collective-permute-done | bytes 524320 | tf_op jit(solution)/shard_map/ppermute | solution.py:390
  19.9 1.9 %add.12 = f32[64,16,128]{2,1,0:T(8,128)} add(f32[64,16,128]{2,1,0:T(8,128)} %get-tuple-element.16, f32[64,16,128]{2,1,0:T(8,128)S(1)} %collective-permute-done) | non-fusion elementwise | flops 131072 | bytes 1572864 | tf_op jit(solution)/shard_map/add | solution.py:390
  21.8 11.2 %all-to-all-start = ((f32[64,16,128]{2,1,0:T(8,128)}), f32[64,16,128]{2,1,0:T(8,128)S(1)}, u32[]{:S(2)}, u32[]{:S(2)}) async-start(f32[64,16,128]{2,1,0:T(8,128)} %add.12), calls=%async_computation | async-start | bytes 1048576 | tf_op jit(solution)/shard_map/all_to_all | solution.py:392
  33.1 11.6 %kinetic0.1.refs_7_ = f32[4,64,4096]{2,1,0:T(8,128)} custom-call(s32[1]{0:T(128)} %bitcast.refs_0_, bf16[384,256]{1,0:T(8,128)(2,1)} %constant.45.clone.refs_1_, bf16[512,256]{1,0:T(8,128)(2,1)} %constant.46.clone.refs_2_, bf16[384,256]{1,0:T(8,128)(2,1)} %constant.47.clone.refs_3_, f32[8,64,4096]{2,1,0:T(8,128)} %refs_4_.4), custom_call_target="tpu_custom_call" | custom-call | flops 6442450944 | bytes 9437184 | tf_op jit(solution)/shard_map/kinetic0/pallas_call | solution.py:369
  44.6 0.4 all-to-all-done
  45.0 0.1 reduce_sum.9
  45.2 0.8 broadcast_in_dim.9
  46.0 9.4 %all-to-all-start.1 = ((f32[64,16,128]{2,1,0:T(8,128)}), f32[64,16,128]{2,1,0:T(8,128)S(1)}, u32[]{:S(2)}, u32[]{:S(2)}) async-start(f32[64,16,128]{2,1,0:T(8,128)} %broadcast_in_dim.9), calls=%async_computation.1 | async-start | bytes 1048576 | tf_op jit(solution)/shard_map/all_to_all | solution.py:397
  55.4 11.6 %kinetic1.1.refs_8_ = f32[4,64,4096]{2,1,0:T(8,128)} custom-call(s32[1]{0:T(128)} %bitcast.refs_0_, bf16[384,256]{1,0:T(8,128)(2,1)} %constant.45.clone.refs_1_, bf16[512,256]{1,0:T(8,128)(2,1)} %constant.46.clone.refs_2_, bf16[384,256]{1,0:T(8,128)(2,1)} %constant.47.clone.refs_3_, f32[8,64,4096]{2,1,0:T(8,128)} %refs_4_.4), custom_call_target="tpu_custom_call" | custom-call | flops 6442450944 | bytes 9437184 | tf_op jit(solution)/shard_map/kinetic1/pallas_call | solution.py:369
  66.9 0.0 all-to-all-done.1.refs_4_
  66.9 0.0 copy-start
  66.9 2.5 %collective-permute-start.1 = (f32[64,16,128]{2,1,0:T(8,128)S(1)}, f32[64,16,128]{2,1,0:T(8,128)S(1)}, u32[]{:S(2)}, u32[]{:S(2)}) collective-permute-start(f32[64,16,128]{2,1,0:T(8,128)S(1)} %all-to-all-done.1.refs_4_), channel_id=1, source_target_pairs={{0,8},{8,0},{1,9},{9,1},{2,10},{10,2},{3,11},{11,3},{4,12},{12,4},... | collective-permute-start | bytes 1572872 | tf_op jit(solution)/shard_map/ppermute | solution.py:399
  69.4 1.5 %collective-permute-done.1.refs_5_ = f32[64,16,128]{2,1,0:T(8,128)S(1)} collective-permute-done((f32[64,16,128]{2,1,0:T(8,128)S(1)}, f32[64,16,128]{2,1,0:T(8,128)S(1)}, u32[]{:S(2)}, u32[]{:S(2)}) %collective-permute-start.1) | collective-permute-done | bytes 524320 | tf_op jit(solution)/shard_map/ppermute | solution.py:399
  71.0 0.0 copy-start.2
  71.0 0.0 copy-done
  71.0 0.8 copy-done.2
  71.7 18.7 %back.1 = f32[8,64,4096]{2,1,0:T(8,128)} custom-call(s32[1]{0:T(128)} %bitcast.refs_0_, bf16[256,256]{1,0:T(8,128)(2,1)} %constant.48.clone.refs_1_, bf16[512,256]{1,0:T(8,128)(2,1)} %constant.49.clone.refs_2_, bf16[256,256]{1,0:T(8,128)(2,1)} %constant.50.clone.refs_3_, f32[64,16,128]{2,1,0:T(8,128)} %copy-done, f32[64,16,128]{2,1,0:T(8,128)} %copy-done.2, ...), custom_call_target="tpu_custom_call" | custom-call | flops 7516192768 | bytes 27262976 | tf_op jit(solution)/shard_map/back/pallas_call | solution.py:351
  (2 shorter events, 0.1 us)
Async XLA Ops:
  0.0 18.2 %copy-start.1 = (f32[4,4096]{1,0:T(4,128)S(1)}, f32[4,4096]{1,0:T(4,128)}, u32[]{:S(2)}) copy-start(f32[4,4096]{1,0:T(4,128)} %param.17) | copy-start | bytes 196612
  16.8 3.1 %collective-permute-start = (f32[64,16,128]{2,1,0:T(8,128)}, f32[64,16,128]{2,1,0:T(8,128)S(1)}, u32[]{:S(2)}, u32[]{:S(2)}) collective-permute-start(f32[64,16,128]{2,1,0:T(8,128)} %get-tuple-element.17), channel_id=1, source_target_pairs={{0,8},{8,0},{1,9},{9,1},{2,10},{10,2},{3,11},{11,3},{4,12},{12,4},... | collective-permute-start | bytes 1572872 | tf_op jit(solution)/shard_map/ppermute | solution.py:390
  21.8 23.2 %all-to-all-start = ((f32[64,16,128]{2,1,0:T(8,128)}), f32[64,16,128]{2,1,0:T(8,128)S(1)}, u32[]{:S(2)}, u32[]{:S(2)}) async-start(f32[64,16,128]{2,1,0:T(8,128)} %add.12), calls=%async_computation | async-start | bytes 1048576 | tf_op jit(solution)/shard_map/all_to_all | solution.py:392
  46.0 20.9 %all-to-all-start.1 = ((f32[64,16,128]{2,1,0:T(8,128)}), f32[64,16,128]{2,1,0:T(8,128)S(1)}, u32[]{:S(2)}, u32[]{:S(2)}) async-start(f32[64,16,128]{2,1,0:T(8,128)} %broadcast_in_dim.9), calls=%async_computation.1 | async-start | bytes 1048576 | tf_op jit(solution)/shard_map/all_to_all | solution.py:397
  66.9 4.0 %copy-start = (f32[64,16,128]{2,1,0:T(8,128)}, f32[64,16,128]{2,1,0:T(8,128)S(1)}, u32[]{:S(2)}) copy-start(f32[64,16,128]{2,1,0:T(8,128)S(1)} %all-to-all-done.1.refs_4_) | copy-start | bytes 1572868
  66.9 4.0 %collective-permute-start.1 = (f32[64,16,128]{2,1,0:T(8,128)S(1)}, f32[64,16,128]{2,1,0:T(8,128)S(1)}, u32[]{:S(2)}, u32[]{:S(2)}) collective-permute-start(f32[64,16,128]{2,1,0:T(8,128)S(1)} %all-to-all-done.1.refs_4_), channel_id=1, source_target_pairs={{0,8},{8,0},{1,9},{9,1},{2,10},{10,2},{3,11},{11,3},{4,12},{12,4},... | collective-permute-start | bytes 1572872 | tf_op jit(solution)/shard_map/ppermute | solution.py:399
  71.0 0.8 copy-start.2
where the time goes:
time: 90.8 us; the launch traced here: 90.4 us
  Pallas kernels  58.6 us (65%)
  starting transfers between devices  24.5 us (27%)
  waiting for transfers between devices  3.64 us (4%)
  other arithmetic  1.99 us (2%)
  local copies, waits for them, and re-layouts  1.66 us (2%)
    pallas_call x2, Pallas kernels, kinetic(): pl.pallas_call(scoped(kinetic_kernel, accs_for(4, 2)), grid=(1,), in_spec...  23.1 us
    pallas_call x1, Pallas kernels, back(): pl.pallas_call(scoped(back_kernel, accs_for(2, 2)), grid=(count // GROUP,...  18.7 us
    pallas_call x1, Pallas kernels, forward(): pl.pallas_call(scoped(forward_kernel, accs_for(2, 2)), grid=(count // GRO...  16.8 us
    all_to_all x1, starting transfers between devices, on_device(): shares = lax.all_to_all(partial, CHIPS, 0, 0, tiled=True)  11.2 us
    all_to_all x1, starting transfers between devices, on_device(): own = lax.all_to_all(copies, CHIPS, 0, 0, tiled=True)  9.38 us
    ppermute x1, starting transfers between devices, on_device(): other = lax.ppermute(own, 'core', SWAP)  2.5 us
    add x1, other arithmetic, on_device(): partial = keep + lax.ppermute(send, 'core', SWAP)  1.9 us
  transfers between devices with their start and end apart: 4, of which 3 were waited for; matrix products, arithmetic and copies ran while one was open for 0% of the time, Pallas kernels for 26%

commit v1 on v0

--- a/solution.py
+++ b/solution.py
@@ -55,7 +55,6 @@
 BF16 = ml_dtypes.bfloat16
 AXES = ("xh", "z", "core", "xl", "y")
 CHIPS = ("xh", "xl", "y", "z")
-PARAMS = dict(vmem_limit_bytes=60 * 2**20)
 UNROLL = 16
 
 
@@ -140,8 +139,10 @@
     return pl.ds(pl.multiple_of(index * size, size), size)
 
 
-def along_tiles(operand, products, accs, target):
+def along_tiles(operand, products, accs, target, before):
     def step(index, _):
+        before(index)
+
         def job(tile, unit, at):
             def finish(*outs):
                 for ref, out in zip(target, outs):
@@ -189,20 +190,28 @@
     return jnp.concatenate(rows, axis=0)
 
 
-def along_x(steps_of, accs, finish_of, after):
+def along_x(steps_of, accs, finish_of, before, after):
     count = UNROLL // 2
 
     def step(index, _):
+        before(index)
+
         def job(block, unit, at):
             return (steps_of(block, unit), [accs[unit][at % 2][0]], functools.partial(finish_of, block, unit))
 
         run([[job(index * count + at, unit, at) for at in range(count)] for unit in range(2)])
-        if after is not None:
-            for at in range(count):
-                after(index * count + at)
+        after(index)
         return 0
 
     lax.fori_loop(0, 16 // count, step, 0)
+
+
+def piece(group, index):
+    return (pl.ds(group * GROUP, GROUP), slice(None), lanes_at(index, UNROLL * 128))
+
+
+def nothing(_):
+    return None
 
 
 def chunks(core):
@@ -213,74 +222,141 @@
         yield position, plane + core * 4, plane + 4 - core * 4, member % 2
 
 
-def forward_kernel(core_ref, occ_ref, z_ref, y_ref, x_ref, orb_ref, val_ref, keep_ref, send_ref, first, second, total, spread, *accs):
-    group = pl.program_id(0)
+def forward_kernel(core_ref, occ_ref, z_ref, y_ref, x_ref, orb_hbm, val_hbm, keep_ref, send_ref, orbs, first, second, total, spread, arrived, left, *accs):
     small, large = ((accs[0:1], accs[1:2]), (accs[2:3], accs[3:4])), (accs[4:6], accs[6:8])
     z_products = [(0, part(z_ref, 0, 128)), (0, part(z_ref, 128, 128))]
     x_products = [(0, part(x_ref, 0, 128)), (0, part(x_ref, 128, 128))]
-    along_tiles(lambda tile: both(orb_ref[:, :, lanes_at(tile, 128)].reshape(ROWS, 128)), z_products, small, [first])
-    along_slow(first, second, y_ref, large)
-
-    @pl.when(group == 0)
-    def _():
-        total[...] = jnp.zeros_like(total)
-
-    def finish(block, pair, out):
-        lanes = lanes_at(block, 256)
-        out = out.reshape(2, N, 256)
-        val_ref[pair * 2 : pair * 2 + 2, :, lanes] = out
-        weighted = [occ_ref[group * GROUP + pair * 2 + one] * (out[one] * out[one]) for one in range(2)]
-        total[:, lanes] = total[:, lanes] + (weighted[0] + weighted[1])
-
-    along_x(lambda block, pair: [(lambda: both(natural(second, block, pair)), True, x_products)], small, finish, None)
-
-    @pl.when(group == pl.num_programs(0) - 1)
-    def _():
-        for tile in range(32):
-            spread[pl.ds(tile, N, stride=32), :] = total[:, tile * 128 : tile * 128 + 128]
-        for position, here, there, half in chunks(core_ref[0]):
-            keep_ref[position] = spread[pl.ds(pl.multiple_of(here * 32 + half * 16, 16), 16), :]
-            send_ref[position] = spread[pl.ds(pl.multiple_of(there * 32 + half * 16, 16), 16), :]
-
-
-def back_kernel(core_ref, z_ref, y_ref, x_ref, own_ref, other_ref, val_ref, kin0_ref, kin1_ref, out_ref, first, second, total, spread, *accs):
-    group = pl.program_id(0)
+
+    def fetch(group, index):
+        return pltpu.make_async_copy(orb_hbm.at[piece(group, index)], orbs.at[piece(group, index)], arrived.at[group, index])
+
+    def give(group, index):
+        return pltpu.make_async_copy(orbs.at[piece(group, index)], val_hbm.at[piece(group, index)], left.at[group, index])
+
+    fetch(0, 0).start()
+    fetch(0, 1).start()
+    total[...] = jnp.zeros_like(total)
+
+    def one_group(group, _):
+        mine = orbs.at[pl.ds(group * GROUP, GROUP)]
+
+        def before(index):
+            fetch(group, index).wait()
+
+            @pl.when(group == 0)
+            def _():
+                fetch(1, index).start()
+
+        along_tiles(lambda tile: both(mine[:, :, lanes_at(tile, 128)].reshape(ROWS, 128)), z_products, small, [first], before)
+        along_slow(first, second, y_ref, large)
+
+        def finish(block, pair, out):
+            lanes = lanes_at(block, 256)
+            out = out.reshape(2, N, 256)
+            mine[pair * 2 : pair * 2 + 2, :, lanes] = out
+            weighted = [occ_ref[group * GROUP + pair * 2 + one] * (out[one] * out[one]) for one in range(2)]
+            total[:, lanes] = total[:, lanes] + (weighted[0] + weighted[1])
+
+        steps = lambda block, pair: [(lambda: both(natural(second, block, pair)), True, x_products)]
+        along_x(steps, small, finish, nothing, lambda index: give(group, index).start())
+        return 0
+
+    lax.fori_loop(0, 2, one_group, 0)
+    for tile in range(32):
+        spread[pl.ds(tile, N, stride=32), :] = total[:, tile * 128 : tile * 128 + 128]
+    for position, here, there, half in chunks(core_ref[0]):
+        keep_ref[position] = spread[pl.ds(pl.multiple_of(here * 32 + half * 16, 16), 16), :]
+        send_ref[position] = spread[pl.ds(pl.multiple_of(there * 32 + half * 16, 16), 16), :]
+    for group in range(2):
+        for index in range(2):
+            give(group, index).wait()
+
+
+def back_kernel(core_ref, z_ref, y_ref, x_ref, own_hbm, other_hbm, val_hbm, kin0_hbm, kin1_hbm, out_hbm, vals, kins, first, second, total, spread, own, other, arrived, kin_arrived, left, halves_arrived, *accs):
     small, large = ((accs[0:1], accs[1:2]), (accs[2:3], accs[3:4])), (accs[4:6], accs[6:8])
     z_products = [(0, part(z_ref, 0, 128)), (0, part(z_ref, 128, 128))]
     x_products = [(0, part(x_ref, 0, 128)), (0, part(x_ref, 128, 128))]
 
-    @pl.when(group == 0)
-    def _():
-        for position, here, there, half in chunks(core_ref[0]):
-            spread[pl.ds(pl.multiple_of(here * 32 + half * 16, 16), 16), :] = own_ref[position]
-            spread[pl.ds(pl.multiple_of(there * 32 + half * 16, 16), 16), :] = other_ref[position]
-        for tile in range(32):
-            total[:, tile * 128 : tile * 128 + 128] = spread[pl.ds(tile, N, stride=32), :]
-
-    def weighted(tile):
-        lanes = lanes_at(tile, 128)
-        return both((val_ref[:, :, lanes] * total[:, lanes][None]).reshape(ROWS, 128))
-
-    along_tiles(weighted, z_products, small, [first])
-    along_slow(first, second, y_ref, large)
-
-    for which, kin_ref in enumerate((kin0_ref, kin1_ref)):
-
-        @pl.when(group == which)
-        def _():
-            def finish(block, pair, out):
-                at = (slice(pair * 2, pair * 2 + 2), slice(None), lanes_at(block, 256))
-                out_ref[at] = out.reshape(2, N, 256) + kin_ref[at]
-
-            along_x(lambda block, pair: [(lambda: both(natural(second, block, pair)), True, x_products)], small, finish, None)
-
-
-def kinetic_kernel(_, z_ref, y_ref, x_ref, orb_ref, out_ref, first, second, *accs):
+    def fetch(group, index):
+        return pltpu.make_async_copy(val_hbm.at[piece(group, index)], vals.at[piece(group, index)], arrived.at[group, index])
+
+    def fetch_kin(which, index):
+        source = (kin0_hbm, kin1_hbm)[which]
+        return pltpu.make_async_copy(source.at[piece(0, index)], kins.at[piece(which, index)], kin_arrived.at[which, index])
+
+    def give(group, index):
+        return pltpu.make_async_copy(vals.at[piece(group, index)], out_hbm.at[piece(group, index)], left.at[group, index])
+
+    pots = [pltpu.make_async_copy(source, target, halves_arrived.at[at]) for at, (source, target) in enumerate(((own_hbm, own), (other_hbm, other)))]
+    for copy in pots:
+        copy.start()
+    fetch(0, 0).start()
+    fetch(0, 1).start()
+    for copy in pots:
+        copy.wait()
+    for position, here, there, half in chunks(core_ref[0]):
+        spread[pl.ds(pl.multiple_of(here * 32 + half * 16, 16), 16), :] = own[position]
+        spread[pl.ds(pl.multiple_of(there * 32 + half * 16, 16), 16), :] = other[position]
+    for tile in range(32):
+        total[:, tile * 128 : tile * 128 + 128] = spread[pl.ds(tile, N, stride=32), :]
+
+    def one_group(group, _):
+        mine, kin = vals.at[pl.ds(group * GROUP, GROUP)], kins.at[pl.ds(group * GROUP, GROUP)]
+
+        def before(index):
+            fetch(group, index).wait()
+            for which in range(2):
+
+                @pl.when(group == which)
+                def _():
+                    fetch_kin(which, index).start()
+                    if which == 0:
+                        fetch(1, index).start()
+
+        def weighted(tile):
+            lanes = lanes_at(tile, 128)
+            return both((mine[:, :, lanes] * total[:, lanes][None]).reshape(ROWS, 128))
+
+        along_tiles(weighted, z_products, small, [first], before)
+        along_slow(first, second, y_ref, large)
+
+        def finish(block, pair, out):
+            at = (slice(pair * 2, pair * 2 + 2), slice(None), lanes_at(block, 256))
+            mine[at] = out.reshape(2, N, 256) + kin[at]
+
+        def before_x(index):
+            for which in range(2):
+
+                @pl.when(group == which)
+                def _():
+                    fetch_kin(which, index).wait()
+
+        steps = lambda block, pair: [(lambda: both(natural(second, block, pair)), True, x_products)]
+        along_x(steps, small, finish, before_x, lambda index: give(group, index).start())
+        return 0
+
+    lax.fori_loop(0, 2, one_group, 0)
+    for group in range(2):
+        for index in range(2):
+            give(group, index).wait()
+
+
+def kinetic_kernel(group, _, z_ref, y_ref, x_ref, orb_hbm, out_hbm, orbs, first, second, arrived, left, *accs):
     small, large = ((accs[0:2], accs[2:4]), (accs[4:6], accs[6:8])), (accs[8:10], accs[10:12])
     z_products = [(0, part(z_ref, 0, 128)), (1, part(z_ref, 128, 128)), (1, part(z_ref, 256, 128))]
     one_products = [(0, part(x_ref, 0, 128))]
     x_products = [(0, part(x_ref, 128, 128)), (0, part(x_ref, 256, 128))]
-    along_tiles(lambda tile: both(orb_ref[:, :, lanes_at(tile, 128)].reshape(ROWS, 128)), z_products, small, [first, second])
+
+    def fetch(index):
+        return pltpu.make_async_copy(orb_hbm.at[piece(group, index)], orbs.at[piece(0, index)], arrived.at[index])
+
+    def give(index):
+        return pltpu.make_async_copy(orbs.at[piece(0, index)], out_hbm.at[piece(0, index)], left.at[index])
+
+    fetch(0).start()
+    fetch(1).start()
+    operand = lambda tile: both(orbs[:, :, lanes_at(tile, 128)].reshape(ROWS, 128))
+    along_tiles(operand, z_products, small, [first, second], lambda index: fetch(index).wait())
     along_slow(first, second, y_ref, large, second)
 
     def steps(block, pair):
@@ -291,13 +367,18 @@
 
     def finish(block, pair, out):
         at = (slice(pair * 2, pair * 2 + 2), slice(None), lanes_at(block, 256))
-        out_ref[at] = out.reshape(2, N, 256) + CENTRE * orb_ref[at]
-
-    along_x(steps, small, finish, None)
+        orbs[at] = out.reshape(2, N, 256) + CENTRE * orbs[at]
+
+    along_x(steps, small, finish, nothing, lambda index: give(index).start())
+    give(0).wait()
+    give(1).wait()
 
 
 SMEM = pl.BlockSpec(memory_space=pltpu.SMEM)
-ORBITALS = pl.BlockSpec((GROUP, N, N * N), lambda group: (group, 0, 0))
+ANY = pl.BlockSpec(memory_space=pl.ANY)
+HBM = pl.BlockSpec(memory_space=pltpu.HBM)
+ALL = pltpu.VMEM((2 * GROUP, N, N * N), jnp.float32)
+QUAD = pltpu.VMEM((GROUP, N, N * N), jnp.float32)
 TURNED = pltpu.VMEM((PAIRS, 16, 8, ROWS), jnp.float32)
 PLANES = pltpu.VMEM((N, N * N), jnp.float32)
 SPREAD = pltpu.VMEM((N * 32, 128), jnp.float32)
@@ -317,7 +398,7 @@
 
 
 def whole(shape):
-    return pl.BlockSpec(shape, lambda *_: (0,) * len(shape), pipeline_mode=pl.Buffered(1))
+    return pl.BlockSpec(shape, lambda *_: (0,) * len(shape))
 
 
 def cost(rows, bytes_accessed):
@@ -328,52 +409,54 @@
     return [whole(table.shape) for table in tables], [jnp.asarray(table) for table in tables]
 
 
+def sems(*shape):
+    return pltpu.SemaphoreType.DMA(shape)
+
+
+def params(mib):
+    return pltpu.CompilerParams(vmem_limit_bytes=mib * 2**20)
+
+
 def forward(core, occupations, orbitals):
-    count = orbitals.shape[0]
     specs, tables = constants(lane_operator(MAGIC, MIXED), slow_operator(MAGIC), lane_operator(MAGIC))
     return pl.pallas_call(
         scoped(forward_kernel, accs_for(2, 2)),
-        grid=(count // GROUP,),
-        in_specs=[SMEM, SMEM, *specs, ORBITALS],
-        out_specs=[ORBITALS, whole(HALF.shape), whole(HALF.shape)],
+        in_specs=[SMEM, SMEM, *specs, HBM],
+        out_specs=[HBM, whole(HALF.shape), whole(HALF.shape)],
         out_shape=[jax.ShapeDtypeStruct(orbitals.shape, jnp.float32), HALF, HALF],
-        scratch_shapes=[TURNED, TURNED, PLANES, SPREAD],
-        compiler_params=pltpu.CompilerParams(**PARAMS),
+        scratch_shapes=[ALL, TURNED, TURNED, PLANES, SPREAD, sems(2, 2), sems(2, 2)],
+        compiler_params=params(52),
         cost_estimate=cost(57344, 18 * 2**20),
         name="forward",
     )(core, occupations, *tables, orbitals)
 
 
 def back(core, own, other, values, kin0, kin1):
-    count = values.shape[0]
     specs, tables = constants(lane_operator(MAGIC.T, MIXED), slow_operator(MAGIC.T), lane_operator(MAGIC.T))
-    quad = whole((GROUP, N, N * N))
+    half = pltpu.VMEM(HALF.shape, jnp.float32)
     return pl.pallas_call(
         scoped(back_kernel, accs_for(2, 2)),
-        grid=(count // GROUP,),
-        in_specs=[SMEM, *specs, whole(HALF.shape), whole(HALF.shape), ORBITALS, quad, quad],
-        out_specs=ORBITALS,
+        in_specs=[SMEM, *specs, ANY, ANY, HBM, HBM, HBM],
+        out_specs=HBM,
         out_shape=jax.ShapeDtypeStruct(values.shape, jnp.float32),
-        scratch_shapes=[TURNED, TURNED, PLANES, SPREAD],
-        compiler_params=pltpu.CompilerParams(**PARAMS),
+        scratch_shapes=[ALL, ALL, TURNED, TURNED, PLANES, SPREAD, half, half, sems(2, 2), sems(2, 2), sems(2, 2), sems(2)],
+        compiler_params=params(52),
         cost_estimate=cost(57344, 26 * 2**20),
         name="back",
     )(core, *tables, own, other, values, kin0, kin1)
 
 
 def kinetic(after, orbitals, group):
-    block = (GROUP, N, N * N)
-    z_table = np.concatenate([ONE_ROWS[MIXED], lane_operator(SIDES, np.arange(128)[MIXED])])
+    z_table = np.concatenate([ONE_ROWS[MIXED], lane_operator(SIDES, MIXED)])
     x_table = np.concatenate([ONE_ROWS, lane_operator(SIDES)])
     specs, tables = constants(z_table, slow_operator(SIDES), x_table)
     return pl.pallas_call(
-        scoped(kinetic_kernel, accs_for(4, 2)),
-        grid=(1,),
-        in_specs=[SMEM, *specs, pl.BlockSpec(block, lambda _: (group, 0, 0))],
-        out_specs=pl.BlockSpec(block, lambda _: (0, 0, 0)),
-        out_shape=jax.ShapeDtypeStruct(block, jnp.float32),
-        scratch_shapes=[TURNED, TURNED],
-        compiler_params=pltpu.CompilerParams(**PARAMS),
+        scoped(functools.partial(kinetic_kernel, group), accs_for(4, 2)),
+        in_specs=[SMEM, *specs, HBM],
+        out_specs=HBM,
+        out_shape=jax.ShapeDtypeStruct((GROUP, N, N * N), jnp.float32),
+        scratch_shapes=[QUAD, TURNED, TURNED, sems(2), sems(2)],
+        compiler_params=params(52),
         cost_estimate=cost(49152, 9 * 2**20),
         name=f"kinetic{group}",
     )(after, *tables, orbitals)

time: 90.8 us -> 84.1 us (0.926)
  Pallas kernels: 58.6 us -> 48.8 us
  waiting for transfers between devices: 3.64 us -> 6.36 us
  local copies, waits for them, and re-layouts: 1.66 us -> 4.32 us
  starting transfers between devices: 24.5 us -> 23.1 us
  other arithmetic: 1.99 us -> 0.95 us
    pallas_call x4, Pallas kernels: 58.6 us -> 48.8 us  [the longest x2 20.1 us: kinetic(): pl.pallas_call(scoped(functools.partial(kinetic_kernel, group), accs_for(...]
    unnamed x6 -> x22, local copies, waits for them, and re-layouts: 0.79 us -> 3.45 us
    all_to_all x1, waiting for transfers between devices: 0.4 us -> 1.91 us  [on_device(): shares = lax.all_to_all(partial, CHIPS, 0, 0, tiled=True)]
    all_to_all x1, starting transfers between devices: 9.38 us -> 7.87 us  [on_device(): own = lax.all_to_all(copies, CHIPS, 0, 0, tiled=True)]
    all_to_all x1, waiting for transfers between devices: 0.01 us -> 1.42 us  [on_device(): own = lax.all_to_all(copies, CHIPS, 0, 0, tiled=True)]
    add x1, other arithmetic: 1.9 us -> 0.86 us  [on_device(): partial = keep + lax.ppermute(send, 'core', SWAP)]
  transfers between devices with their start and end apart: 4 -> 4, of which waited for: 3 -> 4; matrix products, arithmetic and copies ran while one was open for 0% -> 0% of each run, Pallas kernels for 26% -> 24%
where the time goes in v1:
time: 84.1 us; the launch traced here: 83.8 us
  Pallas kernels  48.8 us (58%)
  starting transfers between devices  23.1 us (27%)
  waiting for transfers between devices  6.36 us (8%)
  local copies, waits for them, and re-layouts  4.32 us (5%)
  other arithmetic  0.95 us (1%)
    pallas_call x2, Pallas kernels, kinetic(): pl.pallas_call(scoped(functools.partial(kinetic_kernel, group), accs_for(...  20.1 us
    pallas_call x1, Pallas kernels, forward(): pl.pallas_call(scoped(forward_kernel, accs_for(2, 2)), in_specs=[SMEM, SM...  14.7 us
    pallas_call x1, Pallas kernels, back(): pl.pallas_call(scoped(back_kernel, accs_for(2, 2)), in_specs=[SMEM, *spec...  13.9 us
    all_to_all x1, starting transfers between devices, on_device(): shares = lax.all_to_all(partial, CHIPS, 0, 0, tiled=True)  11.2 us
    all_to_all x1, starting transfers between devices, on_device(): own = lax.all_to_all(copies, CHIPS, 0, 0, tiled=True)  7.87 us
    unnamed x22, local copies, waits for them, and re-layouts  3.45 us
    ppermute x1, starting transfers between devices, on_device(): other = lax.ppermute(own, 'core', SWAP)  2.51 us
    all_to_all x1, waiting for transfers between devices, on_device(): shares = lax.all_to_all(partial, CHIPS, 0, 0, tiled=True)  1.91 us
  transfers between devices with their start and end apart: 4, of which 4 were waited for; matrix products, arithmetic and copies ran while one was open for 0% of the time, Pallas kernels for 24%

profile of v1, /device:TPU:1, one launch (start us, length us, event | category | flops | bytes accessed | tf_op | source)
XLA Modules:
  0.0 83.8 jit_solution(10815045115428827275)
XLA Ops:
  0.0 0.0 copy-start
  0.0 0.7 copy-done
  0.7 0.0 copy-start.3
  0.7 0.9 %copy-done.3 = bf16[512,256]{1,0:T(8,128)(2,1)S(1)} copy-done((bf16[512,256]{1,0:T(8,128)(2,1)S(1)}, bf16[512,256]{1,0:T(8,128)(2,1)}, u32[]{:S(2)}) %copy-start.3) | copy-done | bytes 262168
  1.6 0.0 copy-start.8
  1.6 0.9 %copy-done.8 = bf16[256,256]{1,0:T(8,128)(2,1)S(1)} copy-done((bf16[256,256]{1,0:T(8,128)(2,1)S(1)}, bf16[256,256]{1,0:T(8,128)(2,1)}, u32[]{:S(2)}) %copy-start.8) | copy-done | bytes 131096
  2.5 0.0 copy-start.9
  2.5 0.9 %copy-done.9 = bf16[256,256]{1,0:T(8,128)(2,1)S(1)} copy-done((bf16[256,256]{1,0:T(8,128)(2,1)S(1)}, bf16[256,256]{1,0:T(8,128)(2,1)}, u32[]{:S(2)}) %copy-start.9) | copy-done | bytes 131096
  3.4 0.0 copy-start.10
  3.4 0.0 copy-start.2
  3.4 0.0 copy-start.4
  3.4 0.0 copy-start.5
  3.4 14.7 %forward.1 = (f32[8,64,4096]{2,1,0:T(8,128)}, f32[64,16,128]{2,1,0:T(8,128)S(1)}, f32[64,16,128]{2,1,0:T(8,128)S(1)}) custom-call(s32[1]{0:T(128)} %bitcast.refs_0_, f32[8]{0:T(128)S(1)} %copy-done, bf16[256,256]{1,0:T(8,128)(2,1)S(1)} %copy-done.9, bf16[512,256]{1,0:T(8,128)(2,1)S(1)} %copy-done.3, bf16[256,256]{1,0:T(8,128)(2,1)S(1)} %copy-done.8, ...), custom_call_target="tpu_custom_call" | custom-call | flops 7516192768 | bytes 18874368 | tf_op jit(solution)/shard_map/forward/pallas_call | solution.py:422
  18.2 1.5 %collective-permute-start = (f32[64,16,128]{2,1,0:T(8,128)S(1)}, f32[64,16,128]{2,1,0:T(8,128)S(1)}, u32[]{:S(2)}, u32[]{:S(2)}) collective-permute-start(f32[64,16,128]{2,1,0:T(8,128)S(1)} %get-tuple-element.17), channel_id=1, source_target_pairs={{0,8},{8,0},{1,9},{9,1},{2,10},{10,2},{3,11},{11,3},{4,12},{12,4},... | collective-permute-start | bytes 1572872 | tf_op jit(solution)/shard_map/ppermute | solution.py:473
  19.6 0.0 copy-done.10
  19.7 1.5 %collective-permute-done = f32[64,16,128]{2,1,0:T(8,128)S(1)} collective-permute-done((f32[64,16,128]{2,1,0:T(8,128)S(1)}, f32[64,16,128]{2,1,0:T(8,128)S(1)}, u32[]{:S(2)}, u32[]{:S(2)}) %collective-permute-start) | collective-permute-done | bytes 524320 | tf_op jit(solution)/shard_map/ppermute | solution.py:473
  21.2 0.9 %add.12 = f32[64,16,128]{2,1,0:T(8,128)} add(f32[64,16,128]{2,1,0:T(8,128)S(1)} %get-tuple-element.16, f32[64,16,128]{2,1,0:T(8,128)S(1)} %collective-permute-done) | non-fusion elementwise | flops 131072 | bytes 1572864 | tf_op jit(solution)/shard_map/add | solution.py:473
  22.0 11.2 %all-to-all-start = ((f32[64,16,128]{2,1,0:T(8,128)}), f32[64,16,128]{2,1,0:T(8,128)S(1)}, u32[]{:S(2)}, u32[]{:S(2)}) async-start(f32[64,16,128]{2,1,0:T(8,128)} %add.12), calls=%async_computation | async-start | bytes 1048576 | tf_op jit(solution)/shard_map/all_to_all | solution.py:475
  33.3 0.0 copy-done.2
  33.3 0.0 copy-done.4
  33.3 0.0 copy-done.5
  33.3 10.0 %kinetic0.1.refs_7_ = f32[4,64,4096]{2,1,0:T(8,128)} custom-call(s32[1]{0:T(128)} %bitcast.refs_0_, bf16[384,256]{1,0:T(8,128)(2,1)S(1)} %copy-done.5, bf16[512,256]{1,0:T(8,128)(2,1)S(1)} %copy-done.2, bf16[384,256]{1,0:T(8,128)(2,1)S(1)} %copy-done.4, f32[8,64,4096]{2,1,0:T(8,128)} %refs_4_.4), custom_call_target="tpu_custom_call" | custom-call | flops 6442450944 | bytes 9437184 | tf_op jit(solution)/shard_map/kinetic0/pallas_call | solution.py:453
  43.3 1.9 %all-to-all-done = f32[64,16,128]{2,1,0:T(8,128)S(1)} async-done(((f32[64,16,128]{2,1,0:T(8,128)}), f32[64,16,128]{2,1,0:T(8,128)S(1)}, u32[]{:S(2)}, u32[]{:S(2)}) %all-to-all-start) | async-done | bytes 524320 | tf_op jit(solution)/shard_map/all_to_all | solution.py:475
  45.3 0.1 reduce_sum.9
  45.4 0.8 broadcast_in_dim.9
  46.2 7.9 %all-to-all-start.1 = ((f32[64,16,128]{2,1,0:T(8,128)}), f32[64,16,128]{2,1,0:T(8,128)S(1)}, u32[]{:S(2)}, u32[]{:S(2)}) async-start(f32[64,16,128]{2,1,0:T(8,128)} %broadcast_in_dim.9), calls=%async_computation.1 | async-start | bytes 1048576 | tf_op jit(solution)/shard_map/all_to_all | solution.py:480
  54.1 0.0 copy-start.1
  54.1 0.0 copy-start.6
  54.1 0.0 copy-start.7
  54.1 10.1 %kinetic1.1.refs_8_ = f32[4,64,4096]{2,1,0:T(8,128)} custom-call(s32[1]{0:T(128)} %bitcast.refs_0_, bf16[384,256]{1,0:T(8,128)(2,1)S(1)} %copy-done.5, bf16[512,256]{1,0:T(8,128)(2,1)S(1)} %copy-done.2, bf16[384,256]{1,0:T(8,128)(2,1)S(1)} %copy-done.4, f32[8,64,4096]{2,1,0:T(8,128)} %refs_4_.4), custom_call_target="tpu_custom_call" | custom-call | flops 6442450944 | bytes 9437184 | tf_op jit(solution)/shard_map/kinetic1/pallas_call | solution.py:453
  64.2 1.4 %all-to-all-done.1.refs_4_ = f32[64,16,128]{2,1,0:T(8,128)S(1)} async-done(((f32[64,16,128]{2,1,0:T(8,128)}), f32[64,16,128]{2,1,0:T(8,128)S(1)}, u32[]{:S(2)}, u32[]{:S(2)}) %all-to-all-start.1) | async-done | bytes 524320 | tf_op jit(solution)/shard_map/all_to_all | solution.py:480
  65.6 2.5 %collective-permute-start.1 = (f32[64,16,128]{2,1,0:T(8,128)S(1)}, f32[64,16,128]{2,1,0:T(8,128)S(1)}, u32[]{:S(2)}, u32[]{:S(2)}) collective-permute-start(f32[64,16,128]{2,1,0:T(8,128)S(1)} %all-to-all-done.1.refs_4_), channel_id=1, source_target_pairs={{0,8},{8,0},{1,9},{9,1},{2,10},{10,2},{3,11},{11,3},{4,12},{12,4},... | collective-permute-start | bytes 1572872 | tf_op jit(solution)/shard_map/ppermute | solution.py:482
  68.1 1.5 %collective-permute-done.1.refs_5_ = f32[64,16,128]{2,1,0:T(8,128)S(1)} collective-permute-done((f32[64,16,128]{2,1,0:T(8,128)S(1)}, f32[64,16,128]{2,1,0:T(8,128)S(1)}, u32[]{:S(2)}, u32[]{:S(2)}) %collective-permute-start.1) | collective-permute-done | bytes 524320 | tf_op jit(solution)/shard_map/ppermute | solution.py:482
  69.7 0.0 copy-done.1
  69.7 0.0 copy-done.6
  69.7 0.0 copy-done.7
  69.7 13.9 %back.1 = f32[8,64,4096]{2,1,0:T(8,128)} custom-call(s32[1]{0:T(128)} %bitcast.refs_0_, bf16[256,256]{1,0:T(8,128)(2,1)S(1)} %copy-done.7, bf16[512,256]{1,0:T(8,128)(2,1)S(1)} %copy-done.1, bf16[256,256]{1,0:T(8,128)(2,1)S(1)} %copy-done.6, f32[64,16,128]{2,1,0:T(8,128)S(1)} %all-to-all-done.1.refs_4_, f32[64,16,128]{2,1,0:T(8,128)S(1)} %collective-permute-done.1.refs_5_, ...), custom_call_target="tpu_custom_call" | custom-call | flops 7516192768 | bytes 27262976 | tf_op jit(solution)/shard_map/back/pallas_call | solution.py:437
  (2 shorter events, 0.1 us)
Async XLA Ops:
  0.0 0.7 copy-start
  0.7 0.9 %copy-start.3 = (bf16[512,256]{1,0:T(8,128)(2,1)S(1)}, bf16[512,256]{1,0:T(8,128)(2,1)}, u32[]{:S(2)}) copy-start(bf16[512,256]{1,0:T(8,128)(2,1)} %constant.43.clone.refs_3_) | copy-start | bytes 786436
  1.6 0.9 %copy-start.8 = (bf16[256,256]{1,0:T(8,128)(2,1)S(1)}, bf16[256,256]{1,0:T(8,128)(2,1)}, u32[]{:S(2)}) copy-start(bf16[256,256]{1,0:T(8,128)(2,1)} %constant.44.clone.refs_4_) | copy-start | bytes 393220
  2.5 0.9 %copy-start.9 = (bf16[256,256]{1,0:T(8,128)(2,1)S(1)}, bf16[256,256]{1,0:T(8,128)(2,1)}, u32[]{:S(2)}) copy-start(bf16[256,256]{1,0:T(8,128)(2,1)} %constant.42.clone.refs_2_) | copy-start | bytes 393220
  3.4 16.2 %copy-start.10 = (f32[4,4096]{1,0:T(4,128)S(1)}, f32[4,4096]{1,0:T(4,128)}, u32[]{:S(2)}) copy-start(f32[4,4096]{1,0:T(4,128)} %param.17) | copy-start | bytes 196612
  3.4 29.9 %copy-start.2 = (bf16[512,256]{1,0:T(8,128)(2,1)S(1)}, bf16[512,256]{1,0:T(8,128)(2,1)}, u32[]{:S(2)}) copy-start(bf16[512,256]{1,0:T(8,128)(2,1)} %constant.46.clone.refs_2_) | copy-start | bytes 786436
  3.4 29.9 %copy-start.4 = (bf16[384,256]{1,0:T(8,128)(2,1)S(1)}, bf16[384,256]{1,0:T(8,128)(2,1)}, u32[]{:S(2)}) copy-start(bf16[384,256]{1,0:T(8,128)(2,1)} %constant.47.clone.refs_3_) | copy-start | bytes 589828
  3.4 29.9 %copy-start.5 = (bf16[384,256]{1,0:T(8,128)(2,1)S(1)}, bf16[384,256]{1,0:T(8,128)(2,1)}, u32[]{:S(2)}) copy-start(bf16[384,256]{1,0:T(8,128)(2,1)} %constant.45.clone.refs_1_) | copy-start | bytes 589828
  18.2 3.0 %collective-permute-start = (f32[64,16,128]{2,1,0:T(8,128)S(1)}, f32[64,16,128]{2,1,0:T(8,128)S(1)}, u32[]{:S(2)}, u32[]{:S(2)}) collective-permute-start(f32[64,16,128]{2,1,0:T(8,128)S(1)} %get-tuple-element.17), channel_id=1, source_target_pairs={{0,8},{8,0},{1,9},{9,1},{2,10},{10,2},{3,11},{11,3},{4,12},{12,4},... | collective-permute-start | bytes 1572872 | tf_op jit(solution)/shard_map/ppermute | solution.py:473
  22.0 23.2 %all-to-all-start = ((f32[64,16,128]{2,1,0:T(8,128)}), f32[64,16,128]{2,1,0:T(8,128)S(1)}, u32[]{:S(2)}, u32[]{:S(2)}) async-start(f32[64,16,128]{2,1,0:T(8,128)} %add.12), calls=%async_computation | async-start | bytes 1048576 | tf_op jit(solution)/shard_map/all_to_all | solution.py:475
  46.2 19.4 %all-to-all-start.1 = ((f32[64,16,128]{2,1,0:T(8,128)}), f32[64,16,128]{2,1,0:T(8,128)S(1)}, u32[]{:S(2)}, u32[]{:S(2)}) async-start(f32[64,16,128]{2,1,0:T(8,128)} %broadcast_in_dim.9), calls=%async_computation.1 | async-start | bytes 1048576 | tf_op jit(solution)/shard_map/all_to_all | solution.py:480
  54.1 15.6 %copy-start.1 = (bf16[512,256]{1,0:T(8,128)(2,1)S(1)}, bf16[512,256]{1,0:T(8,128)(2,1)}, u32[]{:S(2)}) copy-start(bf16[512,256]{1,0:T(8,128)(2,1)} %constant.49.clone.refs_2_) | copy-start | bytes 786436
  54.1 15.6 %copy-start.6 = (bf16[256,256]{1,0:T(8,128)(2,1)S(1)}, bf16[256,256]{1,0:T(8,128)(2,1)}, u32[]{:S(2)}) copy-start(bf16[256,256]{1,0:T(8,128)(2,1)} %constant.50.clone.refs_3_) | copy-start | bytes 393220
  54.1 15.6 %copy-start.7 = (bf16[256,256]{1,0:T(8,128)(2,1)S(1)}, bf16[256,256]{1,0:T(8,128)(2,1)}, u32[]{:S(2)}) copy-start(bf16[256,256]{1,0:T(8,128)(2,1)} %constant.48.clone.refs_1_) | copy-start | bytes 393220
  65.6 4.0 %collective-permute-start.1 = (f32[64,16,128]{2,1,0:T(8,128)S(1)}, f32[64,16,128]{2,1,0:T(8,128)S(1)}, u32[]{:S(2)}, u32[]{:S(2)}) collective-permute-start(f32[64,16,128]{2,1,0:T(8,128)S(1)} %all-to-all-done.1.refs_4_), channel_id=1, source_target_pairs={{0,8},{8,0},{1,9},{9,1},{2,10},{10,2},{3,11},{11,3},{4,12},{12,4},... | collective-permute-start | bytes 1572872 | tf_op jit(solution)/shard_map/ppermute | solution.py:482

commit v2 on v1

--- a/solution.py
+++ b/solution.py
@@ -55,7 +55,7 @@
 BF16 = ml_dtypes.bfloat16
 AXES = ("xh", "z", "core", "xl", "y")
 CHIPS = ("xh", "xl", "y", "z")
-UNROLL = 16
+PIECES = 2
 
 
 def circulant(taps, offset):
@@ -139,8 +139,22 @@
     return pl.ds(pl.multiple_of(index * size, size), size)
 
 
-def along_tiles(operand, products, accs, target, before):
-    def step(index, _):
+def repeat(count, body):
+    if count == 1:
+        body(0)
+    else:
+
+        def step(index, _):
+            body(index)
+            return 0
+
+        lax.fori_loop(0, count, step, 0)
+
+
+def along_tiles(loops, operand, products, accs, target, before):
+    count = PAIRS // loops // 2
+
+    def body(index):
         before(index)
 
         def job(tile, unit, at):
@@ -150,14 +164,15 @@
 
             return ([(lambda: operand(tile), True, products)], accs[unit][at % 2], finish)
 
-        run([[job(index * UNROLL + 2 * at + unit, unit, at) for at in range(UNROLL // 2)] for unit in range(2)])
-        return 0
-
-    lax.fori_loop(0, PAIRS // UNROLL, step, 0)
-
-
-def along_slow(source, target, op_ref, accs, add=None):
-    def step(index, _):
+        run([[job((index * count + at) * 2 + unit, unit, at) for at in range(count)] for unit in range(2)])
+
+    repeat(loops, body)
+
+
+def along_slow(loops, source, target, op_ref, accs, add=None):
+    count = 8 // loops
+
+    def body(index):
         def job(block, unit, at):
             cache = []
 
@@ -173,10 +188,9 @@
             second = (lambda: cache[1], False, [(0, part(op_ref, 0, 256))])
             return ([first, second], [accs[unit][at % 2]], finish)
 
-        run([[job(index * 8 + 2 * at + unit, unit, at) for at in range(4)] for unit in range(2)])
-        return 0
-
-    lax.fori_loop(0, 2, step, 0)
+        run([[job((index * count + at) * 2 + unit, unit, at) for at in range(count)] for unit in range(2)])
+
+    repeat(loops, body)
 
 
 def natural(ref, index, pair):
@@ -190,10 +204,10 @@
     return jnp.concatenate(rows, axis=0)
 
 
-def along_x(steps_of, accs, finish_of, before, after):
-    count = UNROLL // 2
-
-    def step(index, _):
+def along_x(loops, steps_of, accs, finish_of, before, after):
+    count = 16 // loops
+
+    def body(index):
         before(index)
 
         def job(block, unit, at):
@@ -201,28 +215,31 @@
 
         run([[job(index * count + at, unit, at) for at in range(count)] for unit in range(2)])
         after(index)
-        return 0
-
-    lax.fori_loop(0, 16 // count, step, 0)
-
-
-def piece(group, index):
-    return (pl.ds(group * GROUP, GROUP), slice(None), lanes_at(index, UNROLL * 128))
+
+    repeat(loops, body)
 
 
 def nothing(_):
     return None
 
 
-def chunks(core):
+def piece(group, index):
+    return (pl.ds(group * GROUP, GROUP), slice(None), lanes_at(index, N * N // PIECES))
+
+
+def places():
     for position in range(64):
         xh, xl, y, z = position // 32, position // 16 % 2, position // 4 % 4, position % 4
-        member = xl * 4 + y
-        plane = xh * 32 + z * 8 + member // 2
-        yield position, plane + core * 4, plane + 4 - core * 4, member % 2
-
-
-def forward_kernel(core_ref, occ_ref, z_ref, y_ref, x_ref, orb_hbm, val_hbm, keep_ref, send_ref, orbs, first, second, total, spread, arrived, left, *accs):
+        for pair in range(2):
+            yield position, (xh * 4 + z) * 8, (xl * 4 + y) * 4 + pair * 2, pair * 8
+
+
+def exchange_halves(low, high):
+    upper = lax.broadcasted_iota(jnp.int32, low.shape, 0) < 4
+    return jnp.where(upper, low, pltpu.roll(high, 4, 0)), jnp.where(upper, pltpu.roll(low, 4, 0), high)
+
+
+def forward_kernel(core_ref, occ_hbm, z_hbm, y_hbm, x_hbm, orb_hbm, val_hbm, keep_ref, send_ref, occ_ref, z_ref, y_ref, x_ref, orbs, first, second, total, ready, arrived, left, *accs):
     small, large = ((accs[0:1], accs[1:2]), (accs[2:3], accs[3:4])), (accs[4:6], accs[6:8])
     z_products = [(0, part(z_ref, 0, 128)), (0, part(z_ref, 128, 128))]
     x_products = [(0, part(x_ref, 0, 128)), (0, part(x_ref, 128, 128))]
@@ -233,9 +250,17 @@
     def give(group, index):
         return pltpu.make_async_copy(orbs.at[piece(group, index)], val_hbm.at[piece(group, index)], left.at[group, index])
 
+    tables = [
+        pltpu.make_async_copy(source, target, ready.at[at])
+        for at, (source, target) in enumerate(((z_hbm, z_ref), (y_hbm, y_ref), (x_hbm, x_ref), (occ_hbm, occ_ref)))
+    ]
+    tables[0].start()
     fetch(0, 0).start()
     fetch(0, 1).start()
+    for table in tables[1:]:
+        table.start()
     total[...] = jnp.zeros_like(total)
+    tables[0].wait()
 
     def one_group(group, _):
         mine = orbs.at[pl.ds(group * GROUP, GROUP)]
@@ -247,8 +272,17 @@
             def _():
                 fetch(1, index).start()
 
-        along_tiles(lambda tile: both(mine[:, :, lanes_at(tile, 128)].reshape(ROWS, 128)), z_products, small, [first], before)
-        along_slow(first, second, y_ref, large)
+        def operand(tile):
+            return both(mine[:, :, lanes_at(tile, 128)].reshape(ROWS, 128))
+
+        along_tiles(2, operand, z_products, small, [first], before)
+
+        @pl.when(group == 0)
+        def _():
+            for table in tables[1:]:
+                table.wait()
+
+        along_slow(1, first, second, y_ref, large)
 
         def finish(block, pair, out):
             lanes = lanes_at(block, 256)
@@ -257,22 +291,22 @@
             weighted = [occ_ref[group * GROUP + pair * 2 + one] * (out[one] * out[one]) for one in range(2)]
             total[:, lanes] = total[:, lanes] + (weighted[0] + weighted[1])
 
-        steps = lambda block, pair: [(lambda: both(natural(second, block, pair)), True, x_products)]
-        along_x(steps, small, finish, nothing, lambda index: give(group, index).start())
+        along_x(2, lambda block, pair: [(lambda: both(natural(second, block, pair)), True, x_products)], small, finish, nothing, lambda index: give(group, index).start())
         return 0
 
     lax.fori_loop(0, 2, one_group, 0)
-    for tile in range(32):
-        spread[pl.ds(tile, N, stride=32), :] = total[:, tile * 128 : tile * 128 + 128]
-    for position, here, there, half in chunks(core_ref[0]):
-        keep_ref[position] = spread[pl.ds(pl.multiple_of(here * 32 + half * 16, 16), 16), :]
-        send_ref[position] = spread[pl.ds(pl.multiple_of(there * 32 + half * 16, 16), 16), :]
+    core = core_ref[0]
+    for position, row, tile, at in places():
+        low, high = [total[row : row + 8, one * 128 : one * 128 + 128] for one in (tile, tile + 1)]
+        zero, one = exchange_halves(low, high)
+        keep_ref[position, at : at + 8, :] = jnp.where(core == 0, zero, one)
+        send_ref[position, at : at + 8, :] = jnp.where(core == 0, one, zero)
     for group in range(2):
-        for index in range(2):
+        for index in range(PIECES):
             give(group, index).wait()
 
 
-def back_kernel(core_ref, z_ref, y_ref, x_ref, own_hbm, other_hbm, val_hbm, kin0_hbm, kin1_hbm, out_hbm, vals, kins, first, second, total, spread, own, other, arrived, kin_arrived, left, halves_arrived, *accs):
+def back_kernel(core_ref, z_hbm, y_hbm, x_hbm, own_hbm, other_hbm, val_hbm, kin0_hbm, kin1_hbm, out_hbm, z_ref, y_ref, x_ref, vals, kins, first, second, total, own, other, ready, arrived, kin_arrived, left, halves_arrived, *accs):
     small, large = ((accs[0:1], accs[1:2]), (accs[2:3], accs[3:4])), (accs[4:6], accs[6:8])
     z_products = [(0, part(z_ref, 0, 128)), (0, part(z_ref, 128, 128))]
     x_products = [(0, part(x_ref, 0, 128)), (0, part(x_ref, 128, 128))]
@@ -288,56 +322,73 @@
         return pltpu.make_async_copy(vals.at[piece(group, index)], out_hbm.at[piece(group, index)], left.at[group, index])
 
     pots = [pltpu.make_async_copy(source, target, halves_arrived.at[at]) for at, (source, target) in enumerate(((own_hbm, own), (other_hbm, other)))]
-    for copy in pots:
+    tables = [
+        pltpu.make_async_copy(source, target, ready.at[at]) for at, (source, target) in enumerate(((z_hbm, z_ref), (y_hbm, y_ref), (x_hbm, x_ref)))
+    ]
+    for copy in pots + tables[:1]:
         copy.start()
     fetch(0, 0).start()
     fetch(0, 1).start()
+    for copy in tables[1:]:
+        copy.start()
     for copy in pots:
         copy.wait()
-    for position, here, there, half in chunks(core_ref[0]):
-        spread[pl.ds(pl.multiple_of(here * 32 + half * 16, 16), 16), :] = own[position]
-        spread[pl.ds(pl.multiple_of(there * 32 + half * 16, 16), 16), :] = other[position]
-    for tile in range(32):
-        total[:, tile * 128 : tile * 128 + 128] = spread[pl.ds(tile, N, stride=32), :]
+    core = core_ref[0]
+    for position, row, tile, at in places():
+        mine, theirs = own[position, at : at + 8, :], other[position, at : at + 8, :]
+        low, high = exchange_halves(jnp.where(core == 0, mine, theirs), jnp.where(core == 0, theirs, mine))
+        total[row : row + 8, tile * 128 : tile * 128 + 128] = low
+        total[row : row + 8, tile * 128 + 128 : tile * 128 + 256] = high
+    tables[0].wait()
 
     def one_group(group, _):
         mine, kin = vals.at[pl.ds(group * GROUP, GROUP)], kins.at[pl.ds(group * GROUP, GROUP)]
 
         def before(index):
             fetch(group, index).wait()
+
+            @pl.when((group == 0) & (index == 0))
+            def _():
+                fetch_kin(0, 0).start()
+                fetch_kin(0, 1).start()
+
+            @pl.when((group == 0) & (index == 1))
+            def _():
+                fetch(1, 0).start()
+                fetch(1, 1).start()
+
+        def operand(tile):
+            lanes = lanes_at(tile, 128)
+            return both((mine[:, :, lanes] * total[:, lanes][None]).reshape(ROWS, 128))
+
+        along_tiles(2, operand, z_products, small, [first], before)
+
+        @pl.when(group == 0)
+        def _():
+            for table in tables[1:]:
+                table.wait()
+
+        along_slow(1, first, second, y_ref, large)
+
+        def before_x(index):
             for which in range(2):
 
                 @pl.when(group == which)
                 def _():
-                    fetch_kin(which, index).start()
+                    fetch_kin(which, index).wait()
                     if which == 0:
-                        fetch(1, index).start()
-
-        def weighted(tile):
-            lanes = lanes_at(tile, 128)
-            return both((mine[:, :, lanes] * total[:, lanes][None]).reshape(ROWS, 128))
-
-        along_tiles(weighted, z_products, small, [first], before)
-        along_slow(first, second, y_ref, large)
+                        fetch_kin(1, index).start()
 
         def finish(block, pair, out):
             at = (slice(pair * 2, pair * 2 + 2), slice(None), lanes_at(block, 256))
             mine[at] = out.reshape(2, N, 256) + kin[at]
 
-        def before_x(index):
-            for which in range(2):
-
-                @pl.when(group == which)
-                def _():
-                    fetch_kin(which, index).wait()
-
-        steps = lambda block, pair: [(lambda: both(natural(second, block, pair)), True, x_products)]
-        along_x(steps, small, finish, before_x, lambda index: give(group, index).start())
+        along_x(2, lambda block, pair: [(lambda: both(natural(second, block, pair)), True, x_products)], small, finish, before_x, lambda index: give(group, index).start())
         return 0
 
     lax.fori_loop(0, 2, one_group, 0)
     for group in range(2):
-        for index in range(2):
+        for index in range(PIECES):
             give(group, index).wait()
 
 
@@ -346,7 +397,6 @@
     z_products = [(0, part(z_ref, 0, 128)), (1, part(z_ref, 128, 128)), (1, part(z_ref, 256, 128))]
     one_products = [(0, part(x_ref, 0, 128))]
     x_products = [(0, part(x_ref, 128, 128)), (0, part(x_ref, 256, 128))]
-
     def fetch(index):
         return pltpu.make_async_copy(orb_hbm.at[piece(group, index)], orbs.at[piece(0, index)], arrived.at[index])
 
@@ -356,8 +406,8 @@
     fetch(0).start()
     fetch(1).start()
     operand = lambda tile: both(orbs[:, :, lanes_at(tile, 128)].reshape(ROWS, 128))
-    along_tiles(operand, z_products, small, [first, second], lambda index: fetch(index).wait())
-    along_slow(first, second, y_ref, large, second)
+    along_tiles(2, operand, z_products, small, [first, second], lambda index: fetch(index).wait())
+    along_slow(1, first, second, y_ref, large, second)
 
     def steps(block, pair):
         return [
@@ -369,7 +419,7 @@
         at = (slice(pair * 2, pair * 2 + 2), slice(None), lanes_at(block, 256))
         orbs[at] = out.reshape(2, N, 256) + CENTRE * orbs[at]
 
-    along_x(steps, small, finish, nothing, lambda index: give(index).start())
+    along_x(2, steps, small, finish, nothing, lambda index: give(index).start())
     give(0).wait()
     give(1).wait()
 
@@ -381,7 +431,6 @@
 QUAD = pltpu.VMEM((GROUP, N, N * N), jnp.float32)
 TURNED = pltpu.VMEM((PAIRS, 16, 8, ROWS), jnp.float32)
 PLANES = pltpu.VMEM((N, N * N), jnp.float32)
-SPREAD = pltpu.VMEM((N * 32, 128), jnp.float32)
 HALF = jax.ShapeDtypeStruct((64, 16, 128), jnp.float32)
 ONE_ROWS = lane_operator(ONE)[:128]
 
@@ -405,6 +454,9 @@
     return pl.CostEstimate(flops=rows * 2 * 256 * 256, bytes_accessed=bytes_accessed, transcendentals=0)
 
 
+TABLES = [pltpu.VMEM((256, 256), jnp.bfloat16), pltpu.VMEM((512, 256), jnp.bfloat16), pltpu.VMEM((256, 256), jnp.bfloat16)]
+
+
 def constants(*tables):
     return [whole(table.shape) for table in tables], [jnp.asarray(table) for table in tables]
 
@@ -418,28 +470,28 @@
 
 
 def forward(core, occupations, orbitals):
-    specs, tables = constants(lane_operator(MAGIC, MIXED), slow_operator(MAGIC), lane_operator(MAGIC))
+    _, tables = constants(lane_operator(MAGIC, MIXED), slow_operator(MAGIC), lane_operator(MAGIC))
     return pl.pallas_call(
         scoped(forward_kernel, accs_for(2, 2)),
-        in_specs=[SMEM, SMEM, *specs, HBM],
+        in_specs=[SMEM, ANY, ANY, ANY, ANY, HBM],
         out_specs=[HBM, whole(HALF.shape), whole(HALF.shape)],
         out_shape=[jax.ShapeDtypeStruct(orbitals.shape, jnp.float32), HALF, HALF],
-        scratch_shapes=[ALL, TURNED, TURNED, PLANES, SPREAD, sems(2, 2), sems(2, 2)],
-        compiler_params=params(52),
+        scratch_shapes=[pltpu.SMEM((2 * GROUP,), jnp.float32), *TABLES, ALL, TURNED, TURNED, PLANES, sems(4), sems(2, PIECES), sems(2, PIECES)],
+        compiler_params=params(60),
         cost_estimate=cost(57344, 18 * 2**20),
         name="forward",
     )(core, occupations, *tables, orbitals)
 
 
 def back(core, own, other, values, kin0, kin1):
-    specs, tables = constants(lane_operator(MAGIC.T, MIXED), slow_operator(MAGIC.T), lane_operator(MAGIC.T))
+    _, tables = constants(lane_operator(MAGIC.T, MIXED), slow_operator(MAGIC.T), lane_operator(MAGIC.T))
     half = pltpu.VMEM(HALF.shape, jnp.float32)
     return pl.pallas_call(
         scoped(back_kernel, accs_for(2, 2)),
-        in_specs=[SMEM, *specs, ANY, ANY, HBM, HBM, HBM],
+        in_specs=[SMEM, ANY, ANY, ANY, ANY, ANY, HBM, HBM, HBM],
         out_specs=HBM,
         out_shape=jax.ShapeDtypeStruct(values.shape, jnp.float32),
-        scratch_shapes=[ALL, ALL, TURNED, TURNED, PLANES, SPREAD, half, half, sems(2, 2), sems(2, 2), sems(2, 2), sems(2)],
+        scratch_shapes=[*TABLES, ALL, ALL, TURNED, TURNED, PLANES, half, half, sems(3), sems(2, PIECES), sems(2, PIECES), sems(2, PIECES), sems(2)],
         compiler_params=params(52),
         cost_estimate=cost(57344, 26 * 2**20),
         name="back",
@@ -455,7 +507,7 @@
         in_specs=[SMEM, *specs, HBM],
         out_specs=HBM,
         out_shape=jax.ShapeDtypeStruct((GROUP, N, N * N), jnp.float32),
-        scratch_shapes=[QUAD, TURNED, TURNED, sems(2), sems(2)],
+        scratch_shapes=[QUAD, TURNED, TURNED, sems(PIECES), sems(PIECES)],
         compiler_params=params(52),
         cost_estimate=cost(49152, 9 * 2**20),
         name=f"kinetic{group}",
@@ -468,7 +520,7 @@
 def on_device(orbitals, occupations, external):
     core = lax.axis_index("core").astype(jnp.int32).reshape(1)
     member = lax.axis_index("xl") * 4 + lax.axis_index("y")
-    own_external = lax.dynamic_index_in_dim(external.reshape(8, 16, 128), member, 0, keepdims=False)
+    own_external = lax.dynamic_index_in_dim(external.reshape(4, 8, 4, 128).transpose(1, 2, 0, 3).reshape(8, 16, 128), member, 0, keepdims=False)
     values, keep, send = forward(core, occupations, orbitals)
     partial = keep + lax.ppermute(send, "core", SWAP)
     partial, after = lax.optimization_barrier((partial, core))

time: 84.1 us -> 81.8 us (0.973)
  local copies, waits for them, and re-layouts: 4.32 us -> 0.98 us
  other arithmetic: 0.95 us -> 1.99 us
    unnamed x22 -> x14, local copies, waits for them, and re-layouts: 3.45 us -> 0.04 us
    add x1, other arithmetic: 0.86 us -> 1.9 us  [on_device(): partial = keep + lax.ppermute(send, 'core', SWAP)]
where the time goes in v2:
time: 81.8 us; the launch traced here: 81.5 us
  Pallas kernels  48.4 us (59%)
  starting transfers between devices  23.1 us (28%)
  waiting for transfers between devices  6.71 us (8%)
  other arithmetic  1.99 us (2%)
  local copies, waits for them, and re-layouts  0.98 us (1%)
    pallas_call x2, Pallas kernels, kinetic(): pl.pallas_call(scoped(functools.partial(kinetic_kernel, group), accs_for(...  19.7 us
    pallas_call x1, Pallas kernels, forward(): pl.pallas_call(scoped(forward_kernel, accs_for(2, 2)), in_specs=[SMEM, AN...  14.8 us
    pallas_call x1, Pallas kernels, back(): pl.pallas_call(scoped(back_kernel, accs_for(2, 2)), in_specs=[SMEM, ANY,...  13.9 us
    all_to_all x1, starting transfers between devices, on_device(): shares = lax.all_to_all(partial, CHIPS, 0, 0, tiled=True)  11.3 us
    all_to_all x1, starting transfers between devices, on_device(): own = lax.all_to_all(copies, CHIPS, 0, 0, tiled=True)  7.87 us
    ppermute x1, starting transfers between devices, on_device(): other = lax.ppermute(own, 'core', SWAP)  2.51 us
    all_to_all x1, waiting for transfers between devices, on_device(): shares = lax.all_to_all(partial, CHIPS, 0, 0, tiled=True)  2.11 us
    add x1, other arithmetic, on_device(): partial = keep + lax.ppermute(send, 'core', SWAP)  1.9 us
  transfers between devices with their start and end apart: 4, of which 4 were waited for; matrix products, arithmetic and copies ran while one was open for 0% of the time, Pallas kernels for 24%

profile of v2, /device:TPU:1, one launch (start us, length us, event | category | flops | bytes accessed | tf_op | source)
XLA Modules:
  0.0 81.5 jit_solution(11043970916157449203)
XLA Ops:
  0.0 0.0 copy-start.6
  0.0 0.0 copy-start.1
  0.0 0.0 copy-start.2
  0.0 0.0 copy-start.3
  0.0 14.8 %forward.1 = (f32[8,64,4096]{2,1,0:T(8,128)}, f32[64,16,128]{2,1,0:T(8,128)}, f32[64,16,128]{2,1,0:T(8,128)}) custom-call(s32[1]{0:T(128)} %bitcast.refs_0_, f32[8]{0:T(128)} %refs_1_.4, bf16[256,256]{1,0:T(8,128)(2,1)} %constant.42.clone.refs_2_, bf16[512,256]{1,0:T(8,128)(2,1)} %constant.43.clone.refs_3_, bf16[256,256]{1,0:T(8,128)(2,1)} %constant.44.clone.refs_4_, ...), custom_call_target="tpu_custom_call" | custom-call | flops 7516192768 | bytes 18874368 | tf_op jit(solution)/shard_map/forward/pallas_call | solution.py:474
  14.8 1.5 %collective-permute-start = (f32[64,16,128]{2,1,0:T(8,128)}, f32[64,16,128]{2,1,0:T(8,128)S(1)}, u32[]{:S(2)}, u32[]{:S(2)}) collective-permute-start(f32[64,16,128]{2,1,0:T(8,128)} %get-tuple-element.17), channel_id=1, source_target_pairs={{0,8},{8,0},{1,9},{9,1},{2,10},{10,2},{3,11},{11,3},{4,12},{12,4},... | collective-permute-start | bytes 1572872 | tf_op jit(solution)/shard_map/ppermute | solution.py:525
  16.3 0.0 copy-done.6
  16.3 0.1 reshape.23
  16.4 1.6 %collective-permute-done = f32[64,16,128]{2,1,0:T(8,128)S(1)} collective-permute-done((f32[64,16,128]{2,1,0:T(8,128)}, f32[64,16,128]{2,1,0:T(8,128)S(1)}, u32[]{:S(2)}, u32[]{:S(2)}) %collective-permute-start) | collective-permute-done | bytes 524320 | tf_op jit(solution)/shard_map/ppermute | solution.py:525
  18.0 1.9 %add.12 = f32[64,16,128]{2,1,0:T(8,128)} add(f32[64,16,128]{2,1,0:T(8,128)} %get-tuple-element.16, f32[64,16,128]{2,1,0:T(8,128)S(1)} %collective-permute-done) | non-fusion elementwise | flops 131072 | bytes 1572864 | tf_op jit(solution)/shard_map/add | solution.py:525
  19.9 11.3 %all-to-all-start = ((f32[64,16,128]{2,1,0:T(8,128)}), f32[64,16,128]{2,1,0:T(8,128)S(1)}, u32[]{:S(2)}, u32[]{:S(2)}) async-start(f32[64,16,128]{2,1,0:T(8,128)} %add.12), calls=%async_computation | async-start | bytes 1048576 | tf_op jit(solution)/shard_map/all_to_all | solution.py:527
  31.2 0.0 copy-done.1
  31.2 0.0 copy-done.2
  31.2 0.0 copy-done.3
  31.2 9.8 %kinetic0.1.refs_7_ = f32[4,64,4096]{2,1,0:T(8,128)} custom-call(s32[1]{0:T(128)} %bitcast.refs_0_, bf16[384,256]{1,0:T(8,128)(2,1)S(1)} %copy-done.3, bf16[512,256]{1,0:T(8,128)(2,1)S(1)} %copy-done.1, bf16[384,256]{1,0:T(8,128)(2,1)S(1)} %copy-done.2, f32[8,64,4096]{2,1,0:T(8,128)} %refs_4_.4), custom_call_target="tpu_custom_call" | custom-call | flops 6442450944 | bytes 9437184 | tf_op jit(solution)/shard_map/kinetic0/pallas_call | solution.py:505
  41.1 2.1 %all-to-all-done = f32[64,16,128]{2,1,0:T(8,128)S(1)} async-done(((f32[64,16,128]{2,1,0:T(8,128)}), f32[64,16,128]{2,1,0:T(8,128)S(1)}, u32[]{:S(2)}, u32[]{:S(2)}) %all-to-all-start) | async-done | bytes 524320 | tf_op jit(solution)/shard_map/all_to_all | solution.py:527
  43.2 0.1 reduce_sum.9
  43.3 0.8 %broadcast_in_dim.9 = f32[64,16,128]{2,1,0:T(8,128)} broadcast(f32[16,128]{1,0:T(8,128)S(1)} %fusion), dimensions={1,2} | broadcast | bytes 532480 | tf_op jit(solution)/shard_map/broadcast_in_dim | solution.py:531
  44.1 7.9 %all-to-all-start.1 = ((f32[64,16,128]{2,1,0:T(8,128)}), f32[64,16,128]{2,1,0:T(8,128)S(1)}, u32[]{:S(2)}, u32[]{:S(2)}) async-start(f32[64,16,128]{2,1,0:T(8,128)} %broadcast_in_dim.9), calls=%async_computation.1 | async-start | bytes 1048576 | tf_op jit(solution)/shard_map/all_to_all | solution.py:532
  52.0 0.0 copy-start
  52.0 0.0 copy-start.4
  52.0 0.0 copy-start.5
  52.0 9.9 %kinetic1.1.refs_8_ = f32[4,64,4096]{2,1,0:T(8,128)} custom-call(s32[1]{0:T(128)} %bitcast.refs_0_, bf16[384,256]{1,0:T(8,128)(2,1)S(1)} %copy-done.3, bf16[512,256]{1,0:T(8,128)(2,1)S(1)} %copy-done.1, bf16[384,256]{1,0:T(8,128)(2,1)S(1)} %copy-done.2, f32[8,64,4096]{2,1,0:T(8,128)} %refs_4_.4), custom_call_target="tpu_custom_call" | custom-call | flops 6442450944 | bytes 9437184 | tf_op jit(solution)/shard_map/kinetic1/pallas_call | solution.py:505
  61.9 1.4 %all-to-all-done.1.refs_4_ = f32[64,16,128]{2,1,0:T(8,128)S(1)} async-done(((f32[64,16,128]{2,1,0:T(8,128)}), f32[64,16,128]{2,1,0:T(8,128)S(1)}, u32[]{:S(2)}, u32[]{:S(2)}) %all-to-all-start.1) | async-done | bytes 524320 | tf_op jit(solution)/shard_map/all_to_all | solution.py:532
  63.4 2.5 %collective-permute-start.1 = (f32[64,16,128]{2,1,0:T(8,128)S(1)}, f32[64,16,128]{2,1,0:T(8,128)S(1)}, u32[]{:S(2)}, u32[]{:S(2)}) collective-permute-start(f32[64,16,128]{2,1,0:T(8,128)S(1)} %all-to-all-done.1.refs_4_), channel_id=1, source_target_pairs={{0,8},{8,0},{1,9},{9,1},{2,10},{10,2},{3,11},{11,3},{4,12},{12,4},... | collective-permute-start | bytes 1572872 | tf_op jit(solution)/shard_map/ppermute | solution.py:534
  65.9 1.5 %collective-permute-done.1.refs_5_ = f32[64,16,128]{2,1,0:T(8,128)S(1)} collective-permute-done((f32[64,16,128]{2,1,0:T(8,128)S(1)}, f32[64,16,128]{2,1,0:T(8,128)S(1)}, u32[]{:S(2)}, u32[]{:S(2)}) %collective-permute-start.1) | collective-permute-done | bytes 524320 | tf_op jit(solution)/shard_map/ppermute | solution.py:534
  67.4 0.0 copy-done
  67.4 0.0 copy-done.4
  67.4 0.0 copy-done.5
  67.4 13.9 %back.1 = f32[8,64,4096]{2,1,0:T(8,128)} custom-call(s32[1]{0:T(128)} %bitcast.refs_0_, bf16[256,256]{1,0:T(8,128)(2,1)S(1)} %copy-done.5, bf16[512,256]{1,0:T(8,128)(2,1)S(1)} %copy-done, bf16[256,256]{1,0:T(8,128)(2,1)S(1)} %copy-done.4, f32[64,16,128]{2,1,0:T(8,128)S(1)} %all-to-all-done.1.refs_4_, f32[64,16,128]{2,1,0:T(8,128)S(1)} %collective-permute-done.1.refs_5_, ...), custom_call_target="tpu_custom_call" | custom-call | flops 7516192768 | bytes 27262976 | tf_op jit(solution)/shard_map/back/pallas_call | solution.py:489
  (2 shorter events, 0.1 us)
Async XLA Ops:
  0.0 16.3 %copy-start.6 = (f32[4,4096]{1,0:T(4,128)S(1)}, f32[4,4096]{1,0:T(4,128)}, u32[]{:S(2)}) copy-start(f32[4,4096]{1,0:T(4,128)} %param.17) | copy-start | bytes 196612
  0.0 31.2 %copy-start.1 = (bf16[512,256]{1,0:T(8,128)(2,1)S(1)}, bf16[512,256]{1,0:T(8,128)(2,1)}, u32[]{:S(2)}) copy-start(bf16[512,256]{1,0:T(8,128)(2,1)} %constant.46.clone.refs_2_) | copy-start | bytes 786436
  0.0 31.2 %copy-start.2 = (bf16[384,256]{1,0:T(8,128)(2,1)S(1)}, bf16[384,256]{1,0:T(8,128)(2,1)}, u32[]{:S(2)}) copy-start(bf16[384,256]{1,0:T(8,128)(2,1)} %constant.47.clone.refs_3_) | copy-start | bytes 589828
  0.0 31.2 %copy-start.3 = (bf16[384,256]{1,0:T(8,128)(2,1)S(1)}, bf16[384,256]{1,0:T(8,128)(2,1)}, u32[]{:S(2)}) copy-start(bf16[384,256]{1,0:T(8,128)(2,1)} %constant.45.clone.refs_1_) | copy-start | bytes 589828
  14.8 3.2 %collective-permute-start = (f32[64,16,128]{2,1,0:T(8,128)}, f32[64,16,128]{2,1,0:T(8,128)S(1)}, u32[]{:S(2)}, u32[]{:S(2)}) collective-permute-start(f32[64,16,128]{2,1,0:T(8,128)} %get-tuple-element.17), channel_id=1, source_target_pairs={{0,8},{8,0},{1,9},{9,1},{2,10},{10,2},{3,11},{11,3},{4,12},{12,4},... | collective-permute-start | bytes 1572872 | tf_op jit(solution)/shard_map/ppermute | solution.py:525
  19.9 23.3 %all-to-all-start = ((f32[64,16,128]{2,1,0:T(8,128)}), f32[64,16,128]{2,1,0:T(8,128)S(1)}, u32[]{:S(2)}, u32[]{:S(2)}) async-start(f32[64,16,128]{2,1,0:T(8,128)} %add.12), calls=%async_computation | async-start | bytes 1048576 | tf_op jit(solution)/shard_map/all_to_all | solution.py:527
  44.1 19.2 %all-to-all-start.1 = ((f32[64,16,128]{2,1,0:T(8,128)}), f32[64,16,128]{2,1,0:T(8,128)S(1)}, u32[]{:S(2)}, u32[]{:S(2)}) async-start(f32[64,16,128]{2,1,0:T(8,128)} %broadcast_in_dim.9), calls=%async_computation.1 | async-start | bytes 1048576 | tf_op jit(solution)/shard_map/all_to_all | solution.py:532
  52.0 15.4 %copy-start = (bf16[512,256]{1,0:T(8,128)(2,1)S(1)}, bf16[512,256]{1,0:T(8,128)(2,1)}, u32[]{:S(2)}) copy-start(bf16[512,256]{1,0:T(8,128)(2,1)} %constant.49.clone.refs_2_) | copy-start | bytes 786436
  52.0 15.4 %copy-start.4 = (bf16[256,256]{1,0:T(8,128)(2,1)S(1)}, bf16[256,256]{1,0:T(8,128)(2,1)}, u32[]{:S(2)}) copy-start(bf16[256,256]{1,0:T(8,128)(2,1)} %constant.50.clone.refs_3_) | copy-start | bytes 393220
  52.0 15.4 %copy-start.5 = (bf16[256,256]{1,0:T(8,128)(2,1)S(1)}, bf16[256,256]{1,0:T(8,128)(2,1)}, u32[]{:S(2)}) copy-start(bf16[256,256]{1,0:T(8,128)(2,1)} %constant.48.clone.refs_1_) | copy-start | bytes 393220
  63.4 4.0 %collective-permute-start.1 = (f32[64,16,128]{2,1,0:T(8,128)S(1)}, f32[64,16,128]{2,1,0:T(8,128)S(1)}, u32[]{:S(2)}, u32[]{:S(2)}) collective-permute-start(f32[64,16,128]{2,1,0:T(8,128)S(1)} %all-to-all-done.1.refs_4_), channel_id=1, source_target_pairs={{0,8},{8,0},{1,9},{9,1},{2,10},{10,2},{3,11},{11,3},{4,12},{12,4},... | collective-permute-start | bytes 1572872 | tf_op jit(solution)/shard_map/ppermute | solution.py:534

commit v3 on v2

--- a/solution.py
+++ b/solution.py
@@ -82,6 +82,14 @@
     return np.concatenate(halves(np.kron(matrix, np.eye(4, dtype=np.float32))))
 
 
+def window_operator(taps):
+    band = np.zeros((16, 32), np.float32)
+    for out in range(16):
+        for position, weight in enumerate(taps):
+            band[out, out + position] = np.float32(weight)
+    return np.concatenate([np.concatenate([part, part], 1) for part in halves(np.kron(band, np.eye(4, dtype=np.float32)))])
+
+
 MAGIC = circulant(MAGIC_TAPS, 8)
 KINETIC = circulant(KINETIC_TAPS, 14) * np.float32(-0.5 / (SPACING * SPACING))
 CENTRE = float(np.float32(3.0) * KINETIC[0, 0])
@@ -204,6 +212,33 @@
     return jnp.concatenate(rows, axis=0)
 
 
+def along_windows(source, target, op_ref, accs):
+    def job(block, unit, at):
+        cache = []
+
+        def window(start):
+            def operand():
+                if not cache:
+                    cache.extend(split(source[:, block].reshape(256, ROWS)))
+                low, high = start * 64 - 32, start * 64 + 96
+                if low < 0:
+                    rows = [(256 + low, 256), (0, high)]
+                elif high > 256:
+                    rows = [(low, 256), (0, high - 256)]
+                else:
+                    rows = [(low, high)]
+                return jnp.concatenate([half[a:b] for half in cache for a, b in rows], axis=0)
+
+            return (operand, False, [(start, part(op_ref, 0, 64)), (start, part(op_ref, 64, 64))])
+
+        def finish(*outs):
+            target[:, block] = jnp.concatenate(outs, axis=0).reshape(PAIRS, 8, ROWS)
+
+        return ([window(start) for start in range(4)], accs[unit][at % 2 * 4 : at % 2 * 4 + 4], finish)
+
+    run([[job(2 * at + unit, unit, at) for at in range(8)] for unit in range(2)])
+
+
 def along_x(loops, steps_of, accs, finish_of, before, after):
     count = 16 // loops
 
@@ -240,7 +275,7 @@
 
 
 def forward_kernel(core_ref, occ_hbm, z_hbm, y_hbm, x_hbm, orb_hbm, val_hbm, keep_ref, send_ref, occ_ref, z_ref, y_ref, x_ref, orbs, first, second, total, ready, arrived, left, *accs):
-    small, large = ((accs[0:1], accs[1:2]), (accs[2:3], accs[3:4])), (accs[4:6], accs[6:8])
+    small, large = ((accs[0:1], accs[1:2]), (accs[2:3], accs[3:4])), (accs[4:12], accs[12:20])
     z_products = [(0, part(z_ref, 0, 128)), (0, part(z_ref, 128, 128))]
     x_products = [(0, part(x_ref, 0, 128)), (0, part(x_ref, 128, 128))]
 
@@ -265,24 +300,21 @@
     def one_group(group, _):
         mine = orbs.at[pl.ds(group * GROUP, GROUP)]
 
-        def before(index):
-            fetch(group, index).wait()
-
-            @pl.when(group == 0)
-            def _():
-                fetch(1, index).start()
-
         def operand(tile):
+            if tile % (PAIRS // PIECES) == 0:
+                fetch(group, tile // (PAIRS // PIECES)).wait()
             return both(mine[:, :, lanes_at(tile, 128)].reshape(ROWS, 128))
 
-        along_tiles(2, operand, z_products, small, [first], before)
+        along_tiles(1, operand, z_products, small, [first], nothing)
 
         @pl.when(group == 0)
         def _():
+            for index in range(PIECES):
+                fetch(1, index).start()
             for table in tables[1:]:
                 table.wait()
 
-        along_slow(1, first, second, y_ref, large)
+        along_windows(first, second, y_ref, large)
 
         def finish(block, pair, out):
             lanes = lanes_at(block, 256)
@@ -307,7 +339,7 @@
 
 
 def back_kernel(core_ref, z_hbm, y_hbm, x_hbm, own_hbm, other_hbm, val_hbm, kin0_hbm, kin1_hbm, out_hbm, z_ref, y_ref, x_ref, vals, kins, first, second, total, own, other, ready, arrived, kin_arrived, left, halves_arrived, *accs):
-    small, large = ((accs[0:1], accs[1:2]), (accs[2:3], accs[3:4])), (accs[4:6], accs[6:8])
+    small, large = ((accs[0:1], accs[1:2]), (accs[2:3], accs[3:4])), (accs[4:12], accs[12:20])
     z_products = [(0, part(z_ref, 0, 128)), (0, part(z_ref, 128, 128))]
     x_products = [(0, part(x_ref, 0, 128)), (0, part(x_ref, 128, 128))]
 
@@ -344,31 +376,24 @@
     def one_group(group, _):
         mine, kin = vals.at[pl.ds(group * GROUP, GROUP)], kins.at[pl.ds(group * GROUP, GROUP)]
 
-        def before(index):
-            fetch(group, index).wait()
-
-            @pl.when((group == 0) & (index == 0))
-            def _():
-                fetch_kin(0, 0).start()
-                fetch_kin(0, 1).start()
-
-            @pl.when((group == 0) & (index == 1))
-            def _():
-                fetch(1, 0).start()
-                fetch(1, 1).start()
-
         def operand(tile):
+            if tile % (PAIRS // PIECES) == 0:
+                fetch(group, tile // (PAIRS // PIECES)).wait()
             lanes = lanes_at(tile, 128)
             return both((mine[:, :, lanes] * total[:, lanes][None]).reshape(ROWS, 128))
 
-        along_tiles(2, operand, z_products, small, [first], before)
+        along_tiles(1, operand, z_products, small, [first], nothing)
 
         @pl.when(group == 0)
         def _():
+            for index in range(PIECES):
+                fetch_kin(0, index).start()
+            for index in range(PIECES):
+                fetch(1, index).start()
             for table in tables[1:]:
                 table.wait()
 
-        along_slow(1, first, second, y_ref, large)
+        along_windows(first, second, y_ref, large)
 
         def before_x(index):
             for which in range(2):
@@ -440,10 +465,7 @@
 
 
 def accs_for(*counts):
-    small, large = counts
-    return [pltpu.ACC(unit)((128, 256), jnp.float32) for unit in range(2) for _ in range(small)] + [
-        pltpu.ACC(unit)((256, 256), jnp.float32) for unit in range(2) for _ in range(large)
-    ]
+    return [pltpu.ACC(unit)((rows, 256), jnp.float32) for rows, count in counts for unit in range(2) for _ in range(count)]
 
 
 def whole(shape):
@@ -454,7 +476,7 @@
     return pl.CostEstimate(flops=rows * 2 * 256 * 256, bytes_accessed=bytes_accessed, transcendentals=0)
 
 
-TABLES = [pltpu.VMEM((256, 256), jnp.bfloat16), pltpu.VMEM((512, 256), jnp.bfloat16), pltpu.VMEM((256, 256), jnp.bfloat16)]
+TABLES = [pltpu.VMEM((256, 256), jnp.bfloat16), pltpu.VMEM((128, 256), jnp.bfloat16), pltpu.VMEM((256, 256), jnp.bfloat16)]
 
 
 def constants(*tables):
@@ -470,9 +492,9 @@
 
 
 def forward(core, occupations, orbitals):
-    _, tables = constants(lane_operator(MAGIC, MIXED), slow_operator(MAGIC), lane_operator(MAGIC))
+    _, tables = constants(lane_operator(MAGIC, MIXED), window_operator(MAGIC_TAPS), lane_operator(MAGIC))
     return pl.pallas_call(
-        scoped(forward_kernel, accs_for(2, 2)),
+        scoped(forward_kernel, accs_for((128, 2), (64, 8))),
         in_specs=[SMEM, ANY, ANY, ANY, ANY, HBM],
         out_specs=[HBM, whole(HALF.shape), whole(HALF.shape)],
         out_shape=[jax.ShapeDtypeStruct(orbitals.shape, jnp.float32), HALF, HALF],
@@ -484,10 +506,10 @@
 
 
 def back(core, own, other, values, kin0, kin1):
-    _, tables = constants(lane_operator(MAGIC.T, MIXED), slow_operator(MAGIC.T), lane_operator(MAGIC.T))
+    _, tables = constants(lane_operator(MAGIC.T, MIXED), window_operator([0.0] + MAGIC_TAPS[::-1]), lane_operator(MAGIC.T))
     half = pltpu.VMEM(HALF.shape, jnp.float32)
     return pl.pallas_call(
-        scoped(back_kernel, accs_for(2, 2)),
+        scoped(back_kernel, accs_for((128, 2), (64, 8))),
         in_specs=[SMEM, ANY, ANY, ANY, ANY, ANY, HBM, HBM, HBM],
         out_specs=HBM,
         out_shape=jax.ShapeDtypeStruct(values.shape, jnp.float32),
@@ -503,7 +525,7 @@
     x_table = np.concatenate([ONE_ROWS, lane_operator(SIDES)])
     specs, tables = constants(z_table, slow_operator(SIDES), x_table)
     return pl.pallas_call(
-        scoped(functools.partial(kinetic_kernel, group), accs_for(4, 2)),
+        scoped(functools.partial(kinetic_kernel, group), accs_for((128, 4), (256, 2))),
         in_specs=[SMEM, *specs, HBM],
         out_specs=HBM,
         out_shape=jax.ShapeDtypeStruct((GROUP, N, N * N), jnp.float32),

time: 81.8 us -> 79 us (0.966)
  Pallas kernels: 48.4 us -> 45.7 us
    pallas_call x2, Pallas kernels: 28.7 us -> 26 us  [the longest x1 13.4 us: forward(): pl.pallas_call(scoped(forward_kernel, accs_for((128, 2), (64, 8))), in_sp...]
  transfers between devices with their start and end apart: 4 -> 4, of which waited for: 4 -> 4; matrix products, arithmetic and copies ran while one was open for 0% -> 0% of each run, Pallas kernels for 24% -> 25%
where the time goes in v3:
time: 79 us; the launch traced here: 78.7 us
  Pallas kernels  45.7 us (58%)
  starting transfers between devices  23.1 us (29%)
  waiting for transfers between devices  6.71 us (8%)
  other arithmetic  1.99 us (3%)
  local copies, waits for them, and re-layouts  0.98 us (1%)
    pallas_call x2, Pallas kernels, kinetic(): pl.pallas_call(scoped(functools.partial(kinetic_kernel, group), accs_for(...  19.7 us
    pallas_call x1, Pallas kernels, forward(): pl.pallas_call(scoped(forward_kernel, accs_for((128, 2), (64, 8))), in_sp...  13.4 us
    pallas_call x1, Pallas kernels, back(): pl.pallas_call(scoped(back_kernel, accs_for((128, 2), (64, 8))), in_specs...  12.5 us
    all_to_all x1, starting transfers between devices, on_device(): shares = lax.all_to_all(partial, CHIPS, 0, 0, tiled=True)  11.3 us
    all_to_all x1, starting transfers between devices, on_device(): own = lax.all_to_all(copies, CHIPS, 0, 0, tiled=True)  7.87 us
    ppermute x1, starting transfers between devices, on_device(): other = lax.ppermute(own, 'core', SWAP)  2.51 us
    all_to_all x1, waiting for transfers between devices, on_device(): shares = lax.all_to_all(partial, CHIPS, 0, 0, tiled=True)  2.11 us
    add x1, other arithmetic, on_device(): partial = keep + lax.ppermute(send, 'core', SWAP)  1.9 us
  transfers between devices with their start and end apart: 4, of which 4 were waited for; matrix products, arithmetic and copies ran while one was open for 0% of the time, Pallas kernels for 25%

profile of v3, /device:TPU:1, one launch (start us, length us, event | category | flops | bytes accessed | tf_op | source)
XLA Modules:
  0.0 78.7 jit_solution(10001889093577018707)
XLA Ops:
  0.0 0.0 copy-start.6
  0.0 0.0 copy-start
  0.0 0.0 copy-start.1
  0.0 0.0 copy-start.2
  0.0 13.4 %forward.1 = (f32[8,64,4096]{2,1,0:T(8,128)}, f32[64,16,128]{2,1,0:T(8,128)}, f32[64,16,128]{2,1,0:T(8,128)}) custom-call(s32[1]{0:T(128)} %bitcast.refs_0_, f32[8]{0:T(128)} %refs_1_.4, bf16[256,256]{1,0:T(8,128)(2,1)} %constant.42.clone.refs_2_, bf16[128,256]{1,0:T(8,128)(2,1)} %constant.43.clone.refs_3_, bf16[256,256]{1,0:T(8,128)(2,1)} %constant.44.clone.refs_4_, ...), custom_call_target="tpu_custom_call" | custom-call | flops 7516192768 | bytes 18874368 | tf_op jit(solution)/shard_map/forward/pallas_call | solution.py:496
  13.5 1.4 %collective-permute-start = (f32[64,16,128]{2,1,0:T(8,128)}, f32[64,16,128]{2,1,0:T(8,128)S(1)}, u32[]{:S(2)}, u32[]{:S(2)}) collective-permute-start(f32[64,16,128]{2,1,0:T(8,128)} %get-tuple-element.17), channel_id=1, source_target_pairs={{0,8},{8,0},{1,9},{9,1},{2,10},{10,2},{3,11},{11,3},{4,12},{12,4},... | collective-permute-start | bytes 1572872 | tf_op jit(solution)/shard_map/ppermute | solution.py:547
  14.9 0.0 copy-done.6
  14.9 0.1 reshape.23
  15.0 1.6 %collective-permute-done = f32[64,16,128]{2,1,0:T(8,128)S(1)} collective-permute-done((f32[64,16,128]{2,1,0:T(8,128)}, f32[64,16,128]{2,1,0:T(8,128)S(1)}, u32[]{:S(2)}, u32[]{:S(2)}) %collective-permute-start) | collective-permute-done | bytes 524320 | tf_op jit(solution)/shard_map/ppermute | solution.py:547
  16.7 1.9 %add.12 = f32[64,16,128]{2,1,0:T(8,128)} add(f32[64,16,128]{2,1,0:T(8,128)} %get-tuple-element.16, f32[64,16,128]{2,1,0:T(8,128)S(1)} %collective-permute-done) | non-fusion elementwise | flops 131072 | bytes 1572864 | tf_op jit(solution)/shard_map/add | solution.py:547
  18.6 11.3 %all-to-all-start = ((f32[64,16,128]{2,1,0:T(8,128)}), f32[64,16,128]{2,1,0:T(8,128)S(1)}, u32[]{:S(2)}, u32[]{:S(2)}) async-start(f32[64,16,128]{2,1,0:T(8,128)} %add.12), calls=%async_computation | async-start | bytes 1048576 | tf_op jit(solution)/shard_map/all_to_all | solution.py:549
  29.8 0.0 copy-done
  29.9 0.0 copy-done.1
  29.9 0.0 copy-done.2
  29.9 9.8 %kinetic0.1.refs_7_ = f32[4,64,4096]{2,1,0:T(8,128)} custom-call(s32[1]{0:T(128)} %bitcast.refs_0_, bf16[384,256]{1,0:T(8,128)(2,1)S(1)} %copy-done.2, bf16[512,256]{1,0:T(8,128)(2,1)S(1)} %copy-done, bf16[384,256]{1,0:T(8,128)(2,1)S(1)} %copy-done.1, f32[8,64,4096]{2,1,0:T(8,128)} %refs_4_.4), custom_call_target="tpu_custom_call" | custom-call | flops 6442450944 | bytes 9437184 | tf_op jit(solution)/shard_map/kinetic0/pallas_call | solution.py:527
  39.7 2.1 %all-to-all-done = f32[64,16,128]{2,1,0:T(8,128)S(1)} async-done(((f32[64,16,128]{2,1,0:T(8,128)}), f32[64,16,128]{2,1,0:T(8,128)S(1)}, u32[]{:S(2)}, u32[]{:S(2)}) %all-to-all-start) | async-done | bytes 524320 | tf_op jit(solution)/shard_map/all_to_all | solution.py:549
  41.8 0.1 reduce_sum.9
  41.9 0.8 %broadcast_in_dim.9 = f32[64,16,128]{2,1,0:T(8,128)} broadcast(f32[16,128]{1,0:T(8,128)S(1)} %fusion), dimensions={1,2} | broadcast | bytes 532480 | tf_op jit(solution)/shard_map/broadcast_in_dim | solution.py:553
  42.8 7.9 %all-to-all-start.1 = ((f32[64,16,128]{2,1,0:T(8,128)}), f32[64,16,128]{2,1,0:T(8,128)S(1)}, u32[]{:S(2)}, u32[]{:S(2)}) async-start(f32[64,16,128]{2,1,0:T(8,128)} %broadcast_in_dim.9), calls=%async_computation.1 | async-start | bytes 1048576 | tf_op jit(solution)/shard_map/all_to_all | solution.py:554
  50.6 0.0 copy-start.3
  50.6 0.0 copy-start.4
  50.7 0.0 copy-start.5
  50.7 9.9 %kinetic1.1.refs_8_ = f32[4,64,4096]{2,1,0:T(8,128)} custom-call(s32[1]{0:T(128)} %bitcast.refs_0_, bf16[384,256]{1,0:T(8,128)(2,1)S(1)} %copy-done.2, bf16[512,256]{1,0:T(8,128)(2,1)S(1)} %copy-done, bf16[384,256]{1,0:T(8,128)(2,1)S(1)} %copy-done.1, f32[8,64,4096]{2,1,0:T(8,128)} %refs_4_.4), custom_call_target="tpu_custom_call" | custom-call | flops 6442450944 | bytes 9437184 | tf_op jit(solution)/shard_map/kinetic1/pallas_call | solution.py:527
  60.6 1.4 %all-to-all-done.1.refs_4_ = f32[64,16,128]{2,1,0:T(8,128)S(1)} async-done(((f32[64,16,128]{2,1,0:T(8,128)}), f32[64,16,128]{2,1,0:T(8,128)S(1)}, u32[]{:S(2)}, u32[]{:S(2)}) %all-to-all-start.1) | async-done | bytes 524320 | tf_op jit(solution)/shard_map/all_to_all | solution.py:554
  62.0 2.5 %collective-permute-start.1 = (f32[64,16,128]{2,1,0:T(8,128)S(1)}, f32[64,16,128]{2,1,0:T(8,128)S(1)}, u32[]{:S(2)}, u32[]{:S(2)}) collective-permute-start(f32[64,16,128]{2,1,0:T(8,128)S(1)} %all-to-all-done.1.refs_4_), channel_id=1, source_target_pairs={{0,8},{8,0},{1,9},{9,1},{2,10},{10,2},{3,11},{11,3},{4,12},{12,4},... | collective-permute-start | bytes 1572872 | tf_op jit(solution)/shard_map/ppermute | solution.py:556
  64.5 1.5 %collective-permute-done.1.refs_5_ = f32[64,16,128]{2,1,0:T(8,128)S(1)} collective-permute-done((f32[64,16,128]{2,1,0:T(8,128)S(1)}, f32[64,16,128]{2,1,0:T(8,128)S(1)}, u32[]{:S(2)}, u32[]{:S(2)}) %collective-permute-start.1) | collective-permute-done | bytes 524320 | tf_op jit(solution)/shard_map/ppermute | solution.py:556
  66.0 0.0 copy-done.3
  66.0 0.0 copy-done.4
  66.0 0.0 copy-done.5
  66.0 12.5 %back.1 = f32[8,64,4096]{2,1,0:T(8,128)} custom-call(s32[1]{0:T(128)} %bitcast.refs_0_, bf16[256,256]{1,0:T(8,128)(2,1)S(1)} %copy-done.4, bf16[128,256]{1,0:T(8,128)(2,1)S(1)} %copy-done.5, bf16[256,256]{1,0:T(8,128)(2,1)S(1)} %copy-done.3, f32[64,16,128]{2,1,0:T(8,128)S(1)} %all-to-all-done.1.refs_4_, f32[64,16,128]{2,1,0:T(8,128)S(1)} %collective-permute-done.1.refs_5_, ...), custom_call_target="tpu_custom_call" | custom-call | flops 7516192768 | bytes 27262976 | tf_op jit(solution)/shard_map/back/pallas_call | solution.py:511
  (2 shorter events, 0.1 us)
Async XLA Ops:
  0.0 14.9 %copy-start.6 = (f32[4,4096]{1,0:T(4,128)S(1)}, f32[4,4096]{1,0:T(4,128)}, u32[]{:S(2)}) copy-start(f32[4,4096]{1,0:T(4,128)} %param.17) | copy-start | bytes 196612
  0.0 29.8 %copy-start = (bf16[512,256]{1,0:T(8,128)(2,1)S(1)}, bf16[512,256]{1,0:T(8,128)(2,1)}, u32[]{:S(2)}) copy-start(bf16[512,256]{1,0:T(8,128)(2,1)} %constant.46.clone.refs_2_) | copy-start | bytes 786436
  0.0 29.8 %copy-start.1 = (bf16[384,256]{1,0:T(8,128)(2,1)S(1)}, bf16[384,256]{1,0:T(8,128)(2,1)}, u32[]{:S(2)}) copy-start(bf16[384,256]{1,0:T(8,128)(2,1)} %constant.47.clone.refs_3_) | copy-start | bytes 589828
  0.0 29.9 %copy-start.2 = (bf16[384,256]{1,0:T(8,128)(2,1)S(1)}, bf16[384,256]{1,0:T(8,128)(2,1)}, u32[]{:S(2)}) copy-start(bf16[384,256]{1,0:T(8,128)(2,1)} %constant.45.clone.refs_1_) | copy-start | bytes 589828
  13.5 3.2 %collective-permute-start = (f32[64,16,128]{2,1,0:T(8,128)}, f32[64,16,128]{2,1,0:T(8,128)S(1)}, u32[]{:S(2)}, u32[]{:S(2)}) collective-permute-start(f32[64,16,128]{2,1,0:T(8,128)} %get-tuple-element.17), channel_id=1, source_target_pairs={{0,8},{8,0},{1,9},{9,1},{2,10},{10,2},{3,11},{11,3},{4,12},{12,4},... | collective-permute-start | bytes 1572872 | tf_op jit(solution)/shard_map/ppermute | solution.py:547
  18.6 23.2 %all-to-all-start = ((f32[64,16,128]{2,1,0:T(8,128)}), f32[64,16,128]{2,1,0:T(8,128)S(1)}, u32[]{:S(2)}, u32[]{:S(2)}) async-start(f32[64,16,128]{2,1,0:T(8,128)} %add.12), calls=%async_computation | async-start | bytes 1048576 | tf_op jit(solution)/shard_map/all_to_all | solution.py:549
  42.8 19.2 %all-to-all-start.1 = ((f32[64,16,128]{2,1,0:T(8,128)}), f32[64,16,128]{2,1,0:T(8,128)S(1)}, u32[]{:S(2)}, u32[]{:S(2)}) async-start(f32[64,16,128]{2,1,0:T(8,128)} %broadcast_in_dim.9), calls=%async_computation.1 | async-start | bytes 1048576 | tf_op jit(solution)/shard_map/all_to_all | solution.py:554
  50.6 15.4 %copy-start.3 = (bf16[256,256]{1,0:T(8,128)(2,1)S(1)}, bf16[256,256]{1,0:T(8,128)(2,1)}, u32[]{:S(2)}) copy-start(bf16[256,256]{1,0:T(8,128)(2,1)} %constant.50.clone.refs_3_) | copy-start | bytes 393220
  50.6 15.4 %copy-start.4 = (bf16[256,256]{1,0:T(8,128)(2,1)S(1)}, bf16[256,256]{1,0:T(8,128)(2,1)}, u32[]{:S(2)}) copy-start(bf16[256,256]{1,0:T(8,128)(2,1)} %constant.48.clone.refs_1_) | copy-start | bytes 393220
  50.7 15.4 %copy-start.5 = (bf16[128,256]{1,0:T(8,128)(2,1)S(1)}, bf16[128,256]{1,0:T(8,128)(2,1)}, u32[]{:S(2)}) copy-start(bf16[128,256]{1,0:T(8,128)(2,1)} %constant.49.clone.refs_2_) | copy-start | bytes 196612
  62.0 4.0 %collective-permute-start.1 = (f32[64,16,128]{2,1,0:T(8,128)S(1)}, f32[64,16,128]{2,1,0:T(8,128)S(1)}, u32[]{:S(2)}, u32[]{:S(2)}) collective-permute-start(f32[64,16,128]{2,1,0:T(8,128)S(1)} %all-to-all-done.1.refs_4_), channel_id=1, source_target_pairs={{0,8},{8,0},{1,9},{9,1},{2,10},{10,2},{3,11},{11,3},{4,12},{12,4},... | collective-permute-start | bytes 1572872 | tf_op jit(solution)/shard_map/ppermute | solution.py:556

commit v4 on v3

--- a/solution.py
+++ b/solution.py
@@ -56,6 +56,7 @@
 AXES = ("xh", "z", "core", "xl", "y")
 CHIPS = ("xh", "xl", "y", "z")
 PIECES = 2
+GIVEN = 4
 
 
 def circulant(taps, offset):
@@ -258,8 +259,8 @@
     return None
 
 
-def piece(group, index):
-    return (pl.ds(group * GROUP, GROUP), slice(None), lanes_at(index, N * N // PIECES))
+def piece(group, index, pieces=PIECES):
+    return (pl.ds(group * GROUP, GROUP), slice(None), lanes_at(index, N * N // pieces))
 
 
 def places():
@@ -283,7 +284,7 @@
         return pltpu.make_async_copy(orb_hbm.at[piece(group, index)], orbs.at[piece(group, index)], arrived.at[group, index])
 
     def give(group, index):
-        return pltpu.make_async_copy(orbs.at[piece(group, index)], val_hbm.at[piece(group, index)], left.at[group, index])
+        return pltpu.make_async_copy(orbs.at[piece(group, index, GIVEN)], val_hbm.at[piece(group, index, GIVEN)], left.at[group, index])
 
     tables = [
         pltpu.make_async_copy(source, target, ready.at[at])
@@ -322,8 +323,10 @@
             mine[pair * 2 : pair * 2 + 2, :, lanes] = out
             weighted = [occ_ref[group * GROUP + pair * 2 + one] * (out[one] * out[one]) for one in range(2)]
             total[:, lanes] = total[:, lanes] + (weighted[0] + weighted[1])
-
-        along_x(2, lambda block, pair: [(lambda: both(natural(second, block, pair)), True, x_products)], small, finish, nothing, lambda index: give(group, index).start())
+            if pair == 1 and block % (16 // GIVEN) == 16 // GIVEN - 1:
+                give(group, block // (16 // GIVEN)).start()
+
+        along_x(1, lambda block, pair: [(lambda: both(natural(second, block, pair)), True, x_products)], small, finish, nothing, nothing)
         return 0
 
     lax.fori_loop(0, 2, one_group, 0)
@@ -334,7 +337,7 @@
         keep_ref[position, at : at + 8, :] = jnp.where(core == 0, zero, one)
         send_ref[position, at : at + 8, :] = jnp.where(core == 0, one, zero)
     for group in range(2):
-        for index in range(PIECES):
+        for index in range(GIVEN):
             give(group, index).wait()
 
 
@@ -351,7 +354,7 @@
         return pltpu.make_async_copy(source.at[piece(0, index)], kins.at[piece(which, index)], kin_arrived.at[which, index])
 
     def give(group, index):
-        return pltpu.make_async_copy(vals.at[piece(group, index)], out_hbm.at[piece(group, index)], left.at[group, index])
+        return pltpu.make_async_copy(vals.at[piece(group, index, GIVEN)], out_hbm.at[piece(group, index, GIVEN)], left.at[group, index])
 
     pots = [pltpu.make_async_copy(source, target, halves_arrived.at[at]) for at, (source, target) in enumerate(((own_hbm, own), (other_hbm, other)))]
     tables = [
@@ -395,25 +398,28 @@
 
         along_windows(first, second, y_ref, large)
 
-        def before_x(index):
+        def before_x(_):
             for which in range(2):
 
                 @pl.when(group == which)
                 def _():
-                    fetch_kin(which, index).wait()
-                    if which == 0:
-                        fetch_kin(1, index).start()
+                    for index in range(PIECES):
+                        fetch_kin(which, index).wait()
+                        if which == 0:
+                            fetch_kin(1, index).start()
 
         def finish(block, pair, out):
             at = (slice(pair * 2, pair * 2 + 2), slice(None), lanes_at(block, 256))
             mine[at] = out.reshape(2, N, 256) + kin[at]
-
-        along_x(2, lambda block, pair: [(lambda: both(natural(second, block, pair)), True, x_products)], small, finish, before_x, lambda index: give(group, index).start())
+            if pair == 1 and block % (16 // GIVEN) == 16 // GIVEN - 1:
+                give(group, block // (16 // GIVEN)).start()
+
+        along_x(1, lambda block, pair: [(lambda: both(natural(second, block, pair)), True, x_products)], small, finish, before_x, nothing)
         return 0
 
     lax.fori_loop(0, 2, one_group, 0)
     for group in range(2):
-        for index in range(PIECES):
+        for index in range(GIVEN):
             give(group, index).wait()
 
 
@@ -498,7 +504,7 @@
         in_specs=[SMEM, ANY, ANY, ANY, ANY, HBM],
         out_specs=[HBM, whole(HALF.shape), whole(HALF.shape)],
         out_shape=[jax.ShapeDtypeStruct(orbitals.shape, jnp.float32), HALF, HALF],
-        scratch_shapes=[pltpu.SMEM((2 * GROUP,), jnp.float32), *TABLES, ALL, TURNED, TURNED, PLANES, sems(4), sems(2, PIECES), sems(2, PIECES)],
+        scratch_shapes=[pltpu.SMEM((2 * GROUP,), jnp.float32), *TABLES, ALL, TURNED, TURNED, PLANES, sems(4), sems(2, PIECES), sems(2, GIVEN)],
         compiler_params=params(60),
         cost_estimate=cost(57344, 18 * 2**20),
         name="forward",
@@ -513,7 +519,7 @@
         in_specs=[SMEM, ANY, ANY, ANY, ANY, ANY, HBM, HBM, HBM],
         out_specs=HBM,
         out_shape=jax.ShapeDtypeStruct(values.shape, jnp.float32),
-        scratch_shapes=[*TABLES, ALL, ALL, TURNED, TURNED, PLANES, half, half, sems(3), sems(2, PIECES), sems(2, PIECES), sems(2, PIECES), sems(2)],
+        scratch_shapes=[*TABLES, ALL, ALL, TURNED, TURNED, PLANES, half, half, sems(3), sems(2, PIECES), sems(2, PIECES), sems(2, GIVEN), sems(2)],
         compiler_params=params(52),
         cost_estimate=cost(57344, 26 * 2**20),
         name="back",

time: 79 us -> 78.1 us (0.989)
  Pallas kernels: 45.7 us -> 44.7 us
where the time goes in v4:
time: 78.1 us; the launch traced here: 77.8 us
  Pallas kernels  44.7 us (57%)
  starting transfers between devices  23.1 us (30%)
  waiting for transfers between devices  6.69 us (9%)
  other arithmetic  1.99 us (3%)
  local copies, waits for them, and re-layouts  0.98 us (1%)
    pallas_call x2, Pallas kernels, kinetic(): pl.pallas_call(scoped(functools.partial(kinetic_kernel, group), accs_for(...  19.7 us
    pallas_call x1, Pallas kernels, forward(): pl.pallas_call(scoped(forward_kernel, accs_for((128, 2), (64, 8))), in_sp...  13.2 us
    pallas_call x1, Pallas kernels, back(): pl.pallas_call(scoped(back_kernel, accs_for((128, 2), (64, 8))), in_specs...  11.8 us
    all_to_all x1, starting transfers between devices, on_device(): shares = lax.all_to_all(partial, CHIPS, 0, 0, tiled=True)  11.3 us
    all_to_all x1, starting transfers between devices, on_device(): own = lax.all_to_all(copies, CHIPS, 0, 0, tiled=True)  7.86 us
    ppermute x1, starting transfers between devices, on_device(): other = lax.ppermute(own, 'core', SWAP)  2.51 us
    all_to_all x1, waiting for transfers between devices, on_device(): shares = lax.all_to_all(partial, CHIPS, 0, 0, tiled=True)  2.1 us
    add x1, other arithmetic, on_device(): partial = keep + lax.ppermute(send, 'core', SWAP)  1.9 us
  transfers between devices with their start and end apart: 4, of which 4 were waited for; matrix products, arithmetic and copies ran while one was open for 0% of the time, Pallas kernels for 25%

profile of v4, /device:TPU:1, one launch (start us, length us, event | category | flops | bytes accessed | tf_op | source)
XLA Modules:
  0.0 77.8 jit_solution(9266219000203557999)
XLA Ops:
  0.0 0.0 copy-start.6
  0.0 0.0 copy-start
  0.0 0.0 copy-start.1
  0.0 0.0 copy-start.2
  0.0 13.2 %forward.1 = (f32[8,64,4096]{2,1,0:T(8,128)}, f32[64,16,128]{2,1,0:T(8,128)}, f32[64,16,128]{2,1,0:T(8,128)}) custom-call(s32[1]{0:T(128)} %bitcast.refs_0_, f32[8]{0:T(128)} %refs_1_.4, bf16[256,256]{1,0:T(8,128)(2,1)} %constant.42.clone.refs_2_, bf16[128,256]{1,0:T(8,128)(2,1)} %constant.43.clone.refs_3_, bf16[256,256]{1,0:T(8,128)(2,1)} %constant.44.clone.refs_4_, ...), custom_call_target="tpu_custom_call" | custom-call | flops 7516192768 | bytes 18874368 | tf_op jit(solution)/shard_map/forward/pallas_call | solution.py:502
  13.3 1.4 %collective-permute-start = (f32[64,16,128]{2,1,0:T(8,128)}, f32[64,16,128]{2,1,0:T(8,128)S(1)}, u32[]{:S(2)}, u32[]{:S(2)}) collective-permute-start(f32[64,16,128]{2,1,0:T(8,128)} %get-tuple-element.17), channel_id=1, source_target_pairs={{0,8},{8,0},{1,9},{9,1},{2,10},{10,2},{3,11},{11,3},{4,12},{12,4},... | collective-permute-start | bytes 1572872 | tf_op jit(solution)/shard_map/ppermute | solution.py:553
  14.7 0.0 copy-done.6
  14.7 0.1 reshape.23
  14.8 1.6 %collective-permute-done = f32[64,16,128]{2,1,0:T(8,128)S(1)} collective-permute-done((f32[64,16,128]{2,1,0:T(8,128)}, f32[64,16,128]{2,1,0:T(8,128)S(1)}, u32[]{:S(2)}, u32[]{:S(2)}) %collective-permute-start) | collective-permute-done | bytes 524320 | tf_op jit(solution)/shard_map/ppermute | solution.py:553
  16.5 1.9 %add.12 = f32[64,16,128]{2,1,0:T(8,128)} add(f32[64,16,128]{2,1,0:T(8,128)} %get-tuple-element.16, f32[64,16,128]{2,1,0:T(8,128)S(1)} %collective-permute-done) | non-fusion elementwise | flops 131072 | bytes 1572864 | tf_op jit(solution)/shard_map/add | solution.py:553
  18.4 11.3 %all-to-all-start = ((f32[64,16,128]{2,1,0:T(8,128)}), f32[64,16,128]{2,1,0:T(8,128)S(1)}, u32[]{:S(2)}, u32[]{:S(2)}) async-start(f32[64,16,128]{2,1,0:T(8,128)} %add.12), calls=%async_computation | async-start | bytes 1048576 | tf_op jit(solution)/shard_map/all_to_all | solution.py:555
  29.6 0.0 copy-done
  29.6 0.0 copy-done.1
  29.7 0.0 copy-done.2
  29.7 9.8 %kinetic0.1.refs_7_ = f32[4,64,4096]{2,1,0:T(8,128)} custom-call(s32[1]{0:T(128)} %bitcast.refs_0_, bf16[384,256]{1,0:T(8,128)(2,1)S(1)} %copy-done.2, bf16[512,256]{1,0:T(8,128)(2,1)S(1)} %copy-done, bf16[384,256]{1,0:T(8,128)(2,1)S(1)} %copy-done.1, f32[8,64,4096]{2,1,0:T(8,128)} %refs_4_.4), custom_call_target="tpu_custom_call" | custom-call | flops 6442450944 | bytes 9437184 | tf_op jit(solution)/shard_map/kinetic0/pallas_call | solution.py:533
  39.5 2.1 %all-to-all-done = f32[64,16,128]{2,1,0:T(8,128)S(1)} async-done(((f32[64,16,128]{2,1,0:T(8,128)}), f32[64,16,128]{2,1,0:T(8,128)S(1)}, u32[]{:S(2)}, u32[]{:S(2)}) %all-to-all-start) | async-done | bytes 524320 | tf_op jit(solution)/shard_map/all_to_all | solution.py:555
  41.6 0.1 reduce_sum.9
  41.7 0.8 %broadcast_in_dim.9 = f32[64,16,128]{2,1,0:T(8,128)} broadcast(f32[16,128]{1,0:T(8,128)S(1)} %fusion), dimensions={1,2} | broadcast | bytes 532480 | tf_op jit(solution)/shard_map/broadcast_in_dim | solution.py:559
  42.5 7.9 %all-to-all-start.1 = ((f32[64,16,128]{2,1,0:T(8,128)}), f32[64,16,128]{2,1,0:T(8,128)S(1)}, u32[]{:S(2)}, u32[]{:S(2)}) async-start(f32[64,16,128]{2,1,0:T(8,128)} %broadcast_in_dim.9), calls=%async_computation.1 | async-start | bytes 1048576 | tf_op jit(solution)/shard_map/all_to_all | solution.py:560
  50.4 0.0 copy-start.3
  50.4 0.0 copy-start.4
  50.4 0.0 copy-start.5
  50.4 9.9 %kinetic1.1.refs_8_ = f32[4,64,4096]{2,1,0:T(8,128)} custom-call(s32[1]{0:T(128)} %bitcast.refs_0_, bf16[384,256]{1,0:T(8,128)(2,1)S(1)} %copy-done.2, bf16[512,256]{1,0:T(8,128)(2,1)S(1)} %copy-done, bf16[384,256]{1,0:T(8,128)(2,1)S(1)} %copy-done.1, f32[8,64,4096]{2,1,0:T(8,128)} %refs_4_.4), custom_call_target="tpu_custom_call" | custom-call | flops 6442450944 | bytes 9437184 | tf_op jit(solution)/shard_map/kinetic1/pallas_call | solution.py:533
  60.3 1.4 %all-to-all-done.1.refs_4_ = f32[64,16,128]{2,1,0:T(8,128)S(1)} async-done(((f32[64,16,128]{2,1,0:T(8,128)}), f32[64,16,128]{2,1,0:T(8,128)S(1)}, u32[]{:S(2)}, u32[]{:S(2)}) %all-to-all-start.1) | async-done | bytes 524320 | tf_op jit(solution)/shard_map/all_to_all | solution.py:560
  61.8 2.5 %collective-permute-start.1 = (f32[64,16,128]{2,1,0:T(8,128)S(1)}, f32[64,16,128]{2,1,0:T(8,128)S(1)}, u32[]{:S(2)}, u32[]{:S(2)}) collective-permute-start(f32[64,16,128]{2,1,0:T(8,128)S(1)} %all-to-all-done.1.refs_4_), channel_id=1, source_target_pairs={{0,8},{8,0},{1,9},{9,1},{2,10},{10,2},{3,11},{11,3},{4,12},{12,4},... | collective-permute-start | bytes 1572872 | tf_op jit(solution)/shard_map/ppermute | solution.py:562
  64.3 1.5 %collective-permute-done.1.refs_5_ = f32[64,16,128]{2,1,0:T(8,128)S(1)} collective-permute-done((f32[64,16,128]{2,1,0:T(8,128)S(1)}, f32[64,16,128]{2,1,0:T(8,128)S(1)}, u32[]{:S(2)}, u32[]{:S(2)}) %collective-permute-start.1) | collective-permute-done | bytes 524320 | tf_op jit(solution)/shard_map/ppermute | solution.py:562
  65.8 0.0 copy-done.3
  65.8 0.0 copy-done.4
  65.8 0.0 copy-done.5
  65.8 11.8 %back.1 = f32[8,64,4096]{2,1,0:T(8,128)} custom-call(s32[1]{0:T(128)} %bitcast.refs_0_, bf16[256,256]{1,0:T(8,128)(2,1)S(1)} %copy-done.4, bf16[128,256]{1,0:T(8,128)(2,1)S(1)} %copy-done.5, bf16[256,256]{1,0:T(8,128)(2,1)S(1)} %copy-done.3, f32[64,16,128]{2,1,0:T(8,128)S(1)} %all-to-all-done.1.refs_4_, f32[64,16,128]{2,1,0:T(8,128)S(1)} %collective-permute-done.1.refs_5_, ...), custom_call_target="tpu_custom_call" | custom-call | flops 7516192768 | bytes 27262976 | tf_op jit(solution)/shard_map/back/pallas_call | solution.py:517
  (2 shorter events, 0.1 us)
Async XLA Ops:
  0.0 14.7 %copy-start.6 = (f32[4,4096]{1,0:T(4,128)S(1)}, f32[4,4096]{1,0:T(4,128)}, u32[]{:S(2)}) copy-start(f32[4,4096]{1,0:T(4,128)} %param.17) | copy-start | bytes 196612
  0.0 29.6 %copy-start = (bf16[512,256]{1,0:T(8,128)(2,1)S(1)}, bf16[512,256]{1,0:T(8,128)(2,1)}, u32[]{:S(2)}) copy-start(bf16[512,256]{1,0:T(8,128)(2,1)} %constant.46.clone.refs_2_) | copy-start | bytes 786436
  0.0 29.6 %copy-start.1 = (bf16[384,256]{1,0:T(8,128)(2,1)S(1)}, bf16[384,256]{1,0:T(8,128)(2,1)}, u32[]{:S(2)}) copy-start(bf16[384,256]{1,0:T(8,128)(2,1)} %constant.47.clone.refs_3_) | copy-start | bytes 589828
  0.0 29.6 %copy-start.2 = (bf16[384,256]{1,0:T(8,128)(2,1)S(1)}, bf16[384,256]{1,0:T(8,128)(2,1)}, u32[]{:S(2)}) copy-start(bf16[384,256]{1,0:T(8,128)(2,1)} %constant.45.clone.refs_1_) | copy-start | bytes 589828
  13.3 3.2 %collective-permute-start = (f32[64,16,128]{2,1,0:T(8,128)}, f32[64,16,128]{2,1,0:T(8,128)S(1)}, u32[]{:S(2)}, u32[]{:S(2)}) collective-permute-start(f32[64,16,128]{2,1,0:T(8,128)} %get-tuple-element.17), channel_id=1, source_target_pairs={{0,8},{8,0},{1,9},{9,1},{2,10},{10,2},{3,11},{11,3},{4,12},{12,4},... | collective-permute-start | bytes 1572872 | tf_op jit(solution)/shard_map/ppermute | solution.py:553
  18.4 23.2 %all-to-all-start = ((f32[64,16,128]{2,1,0:T(8,128)}), f32[64,16,128]{2,1,0:T(8,128)S(1)}, u32[]{:S(2)}, u32[]{:S(2)}) async-start(f32[64,16,128]{2,1,0:T(8,128)} %add.12), calls=%async_computation | async-start | bytes 1048576 | tf_op jit(solution)/shard_map/all_to_all | solution.py:555
  42.5 19.2 %all-to-all-start.1 = ((f32[64,16,128]{2,1,0:T(8,128)}), f32[64,16,128]{2,1,0:T(8,128)S(1)}, u32[]{:S(2)}, u32[]{:S(2)}) async-start(f32[64,16,128]{2,1,0:T(8,128)} %broadcast_in_dim.9), calls=%async_computation.1 | async-start | bytes 1048576 | tf_op jit(solution)/shard_map/all_to_all | solution.py:560
  50.4 15.4 %copy-start.3 = (bf16[256,256]{1,0:T(8,128)(2,1)S(1)}, bf16[256,256]{1,0:T(8,128)(2,1)}, u32[]{:S(2)}) copy-start(bf16[256,256]{1,0:T(8,128)(2,1)} %constant.50.clone.refs_3_) | copy-start | bytes 393220
  50.4 15.4 %copy-start.4 = (bf16[256,256]{1,0:T(8,128)(2,1)S(1)}, bf16[256,256]{1,0:T(8,128)(2,1)}, u32[]{:S(2)}) copy-start(bf16[256,256]{1,0:T(8,128)(2,1)} %constant.48.clone.refs_1_) | copy-start | bytes 393220
  50.4 15.4 %copy-start.5 = (bf16[128,256]{1,0:T(8,128)(2,1)S(1)}, bf16[128,256]{1,0:T(8,128)(2,1)}, u32[]{:S(2)}) copy-start(bf16[128,256]{1,0:T(8,128)(2,1)} %constant.49.clone.refs_2_) | copy-start | bytes 196612
  61.8 4.0 %collective-permute-start.1 = (f32[64,16,128]{2,1,0:T(8,128)S(1)}, f32[64,16,128]{2,1,0:T(8,128)S(1)}, u32[]{:S(2)}, u32[]{:S(2)}) collective-permute-start(f32[64,16,128]{2,1,0:T(8,128)S(1)} %all-to-all-done.1.refs_4_), channel_id=1, source_target_pairs={{0,8},{8,0},{1,9},{9,1},{2,10},{10,2},{3,11},{11,3},{4,12},{12,4},... | collective-permute-start | bytes 1572872 | tf_op jit(solution)/shard_map/ppermute | solution.py:562
